TPU v7x, 512 devices: a whole 4x8x8 slice. The times are simulated.
512 devices in a mesh: wide: 64 (over x, y, z_hi), lane: 8 (over z_lo, core).
Axes of the slice: x: 4, y: 8, z: 8 (z_hi: 2, z_lo: 4; z = z_hi * 4 + z_lo), core: 2. Of those that a mesh axis runs over, the one named last changes fastest.
Arguments:
- source: float32 [131072, 256], P(('wide', 'lane')), may hold values from -80 to 80
- target: float32 [65536, 256], P(('wide', 'lane')), may hold values from -80 to 80
- observed: float32 [2, 131072, 128], P(None, ('wide', 'lane')), may hold values from -15 to 15
- tiles: int32 [2, 1024, 1], P(None, ('wide', 'lane')), may hold values 0 or 1
Outputs:
- new_source: float32 [131072, 256], P(('wide', 'lane'))
- carried_target: float32 [65536, 256], P(('wide', 'lane'))
All inputs are finite; a program needn't handle non-finite values. No bound on the sum of `tiles` on one device may be relied on, other than what follows from the above.
Results may differ from a plain program's by a relative error of at most 0.00026.
Values sent between devices are 32-bit elements; how exact they have to be, the bound alone decides.
No kernel may reach another device: no remote copies, remote signals or barrier semaphores. Data moves between devices by JAX's collectives and lax.ppermute only.
A program may use at most 64 MiB of HBM per device.

v0:
```python
import jax
import jax.numpy as jnp
from jax import lax
from jax.sharding import PartitionSpec as P

VISITS = 2


step_size = 0.0002


def shifted(value, axis, steps):
    count = lax.axis_size(axis)
    pairs = [(source, (source + steps) % count) for source in range(count)]
    return lax.ppermute(value, axis, pairs)


def solve_right(gradient, factor):
    partial_value = lax.linalg.triangular_solve(
        factor, gradient, left_side=False, lower=True, transpose_a=True
    )
    return lax.linalg.triangular_solve(factor, partial_value, left_side=False, lower=True)


def cross_product(left, right):
    return lax.dot_general(left, right, (((0,), (0,)), ((), ())), precision=lax.Precision.HIGHEST)


def on_device(source, target, observed, tiles):
    highest = lax.Precision.HIGHEST
    devices = lax.axis_size("wide") * lax.axis_size("lane")
    source_rows = source.shape[0] * devices
    target_rows = target.shape[0] * devices
    tile_rows = source.shape[0] // tiles.shape[1]
    gram_source, gram_target = lax.psum(
        (cross_product(source, source), cross_product(target, target)), ("wide", "lane")
    )
    gram_source = gram_source / source_rows
    gram_target = gram_target / target_rows
    for visit_number in range(VISITS):
        factor_source = jnp.linalg.cholesky(gram_source)
        factor_target = jnp.linalg.cholesky(gram_target)
        expanded = jnp.repeat(
            jnp.repeat(tiles[visit_number].astype(jnp.float32), tile_rows, axis=0),
            tile_rows,
            axis=1,
        )
        predicted = lax.dot_general(source, target, (((1,), (1,)), ((), ())), precision=highest)
        residual = expanded * (predicted - observed[visit_number])
        grad_source = jnp.dot(residual, target, precision=highest)
        grad_target = cross_product(residual, source)
        step_source = solve_right(grad_source, factor_target)
        step_target = solve_right(grad_target, factor_source)
        remaining = visit_number + 1 < VISITS
        source = source - step_size * step_source
        target = target - step_size * step_target
        if remaining:
            gram_source, gram_target = lax.psum(
                (cross_product(source, source), cross_product(target, target)), ("wide", "lane")
            )
            gram_source = gram_source / source_rows
            gram_target = gram_target / target_rows
        target = shifted(target, "wide", 1)
    return (source, target)


def solution(mesh):
    placed = (
        P(("wide", "lane"), None),
        P(("wide", "lane"), None),
        P(None, ("wide", "lane"), None),
        P(None, ("wide", "lane"), None),
    )
    return jax.shard_map(
        on_device,
        mesh=mesh,
        in_specs=placed,
        out_specs=(P(("wide", "lane"), None), P(("wide", "lane"), None)),
        check_vma=False,
    )
```

profile of v0, /device:TPU:1, one launch (start us, length us, event | category | flops | bytes accessed | tf_op | source)
XLA Modules:
  0.0 848.0 jit_solution(12258565601219756670)
XLA Ops:
  7.2 2.1 fusion.55
  13.1 279.2 %all-reduce.8.cloned.1.call-done = (f32[256,256]{0,1:T(8,128)}, f32[256,256]{0,1:T(8,128)}) async-done(((f32[256,256]{0,1:T(8,128)}, f32[256,256]{0,1:T(8,128)}), (f32[256,256]{0,1:T(8,128)}, f32[256,256]{0,1:T(8,128)})) %all-reduce.8.cloned.1.call-update) | async-done | bytes 524304 | tf_op jit(solution)/shard_map/psum | solution.py:35
  295.3 11.7 %cholesky.248 = f32[128,128]{1,0:T(8,128)S(1)} custom-call(f32[128,128]{1,0:T(8,128)S(1)} %cholesky.349), custom_call_target="Cholesky" | custom-call | tf_op jit(solution)/shard_map/jit(cholesky)/cholesky | solution.py:41
  307.1 9.8 %custom-call.30 = f32[1,128,128]{1,2,0:T(8,128)S(1)} custom-call(f32[1,128,128]{2,1,0:T(8,128)S(1)} %get-tuple-element.128), custom_call_target="InvertDiagBlocksLowerTriangular" | custom-call | tf_op jit(solution)/shard_map/jit(cholesky)/cholesky | solution.py:41
  317.4 11.7 %cholesky.265 = f32[128,128]{1,0:T(8,128)S(1)} custom-call(f32[128,128]{1,0:T(8,128)S(1)} %convolution_subtract_fusion.11), custom_call_target="Cholesky" | custom-call | tf_op jit(solution)/shard_map/jit(cholesky)/cholesky | solution.py:41
  332.0 4.4 while.17
  332.9 1.4 bitcast_dynamic-update-slice_fusion.9
  334.9 1.4 bitcast_dynamic-update-slice_fusion.9
  336.4 19.7 %custom-call.31 = f32[2,128,128]{1,2,0:T(8,128)S(1)} custom-call(f32[2,128,128]{2,1,0:T(8,128)S(1)} %get-tuple-element.65), custom_call_target="InvertDiagBlocksLowerTriangular" | custom-call | tf_op jit(solution)/shard_map/triangular_solve/custom-call.5 | solution.py:19
  357.7 11.7 %cholesky.214 = f32[128,128]{1,0:T(8,128)S(1)} custom-call(f32[128,128]{1,0:T(8,128)S(1)} %cholesky.346), custom_call_target="Cholesky" | custom-call | tf_op jit(solution)/shard_map/jit(cholesky)/cholesky | solution.py:42
  369.4 9.8 %custom-call.27 = f32[1,128,128]{1,2,0:T(8,128)S(1)} custom-call(f32[1,128,128]{2,1,0:T(8,128)S(1)} %get-tuple-element.132), custom_call_target="InvertDiagBlocksLowerTriangular" | custom-call | tf_op jit(solution)/shard_map/jit(cholesky)/cholesky | solution.py:42
  379.7 11.7 %cholesky.231 = f32[128,128]{1,0:T(8,128)S(1)} custom-call(f32[128,128]{1,0:T(8,128)S(1)} %convolution_subtract_fusion.12), custom_call_target="Cholesky" | custom-call | tf_op jit(solution)/shard_map/jit(cholesky)/cholesky | solution.py:42
  394.2 4.1 while.16
  394.9 1.4 bitcast_dynamic-update-slice_fusion.8
  396.9 1.4 bitcast_dynamic-update-slice_fusion.8
  398.3 31.0 %custom-call.28 = f32[2,128,128]{1,2,0:T(8,128)S(1)} custom-call(f32[2,128,128]{2,1,0:T(8,128)S(1)} %get-tuple-element.63), custom_call_target="InvertDiagBlocksLowerTriangular" | custom-call | tf_op jit(solution)/shard_map/triangular_solve/custom-call.0 | solution.py:19
  432.4 3.5 collective-permute-start
  437.0 13.4 %collective-permute-done = f32[128,256]{0,1:T(8,128)S(1)} collective-permute-done((f32[128,256]{0,1:T(8,128)S(1)}, f32[128,256]{0,1:T(8,128)S(1)}, u32[]{:S(2)}, u32[]{:S(2)}) %collective-permute-start) | collective-permute-done | bytes 131104 | tf_op jit(solution)/shard_map/ppermute | solution.py:15
  451.8 257.3 %all-reduce.6.cloned.1.call-done = (f32[256,256]{0,1:T(8,128)}, f32[256,256]{0,1:T(8,128)}) async-done(((f32[256,256]{0,1:T(8,128)}, f32[256,256]{0,1:T(8,128)}), (f32[256,256]{0,1:T(8,128)}, f32[256,256]{0,1:T(8,128)})) %all-reduce.6.cloned.1.call-update) | async-done | bytes 524304 | tf_op jit(solution)/shard_map/psum | solution.py:58
  711.0 11.7 %cholesky.316 = f32[128,128]{1,0:T(8,128)S(1)} custom-call(f32[128,128]{1,0:T(8,128)S(1)} %cholesky.355), custom_call_target="Cholesky" | custom-call | tf_op jit(solution)/shard_map/jit(cholesky)/cholesky | solution.py:41
  722.8 9.8 %custom-call.36 = f32[1,128,128]{1,2,0:T(8,128)S(1)} custom-call(f32[1,128,128]{2,1,0:T(8,128)S(1)} %get-tuple-element.120), custom_call_target="InvertDiagBlocksLowerTriangular" | custom-call | tf_op jit(solution)/shard_map/jit(cholesky)/cholesky | solution.py:41
  733.1 11.7 %cholesky.333 = f32[128,128]{1,0:T(8,128)S(1)} custom-call(f32[128,128]{1,0:T(8,128)S(1)} %convolution_subtract_fusion.7), custom_call_target="Cholesky" | custom-call | tf_op jit(solution)/shard_map/jit(cholesky)/cholesky | solution.py:41
  747.5 4.2 while.19
  748.3 1.4 bitcast_dynamic-update-slice_fusion.11
  750.3 1.4 bitcast_dynamic-update-slice_fusion.11
  751.7 19.7 %custom-call.37 = f32[2,128,128]{1,2,0:T(8,128)S(1)} custom-call(f32[2,128,128]{2,1,0:T(8,128)S(1)} %get-tuple-element.69), custom_call_target="InvertDiagBlocksLowerTriangular" | custom-call | tf_op jit(solution)/shard_map/triangular_solve/custom-call.5 | solution.py:19
  773.0 3.5 collective-permute-start.1
  776.7 11.7 %cholesky.282 = f32[128,128]{1,0:T(8,128)S(1)} custom-call(f32[128,128]{1,0:T(8,128)S(1)} %cholesky.352), custom_call_target="Cholesky" | custom-call | tf_op jit(solution)/shard_map/jit(cholesky)/cholesky | solution.py:42
  788.5 9.8 %custom-call.33 = f32[1,128,128]{1,2,0:T(8,128)S(1)} custom-call(f32[1,128,128]{2,1,0:T(8,128)S(1)} %get-tuple-element.124), custom_call_target="InvertDiagBlocksLowerTriangular" | custom-call | tf_op jit(solution)/shard_map/jit(cholesky)/cholesky | solution.py:42
  798.8 11.7 %cholesky.299 = f32[128,128]{1,0:T(8,128)S(1)} custom-call(f32[128,128]{1,0:T(8,128)S(1)} %convolution_subtract_fusion.8), custom_call_target="Cholesky" | custom-call | tf_op jit(solution)/shard_map/jit(cholesky)/cholesky | solution.py:42
  813.2 4.3 while.18
  817.4 19.7 %custom-call.34 = f32[2,128,128]{1,2,0:T(8,128)S(1)} custom-call(f32[2,128,128]{2,1,0:T(8,128)S(1)} %get-tuple-element.67), custom_call_target="InvertDiagBlocksLowerTriangular" | custom-call | tf_op jit(solution)/shard_map/triangular_solve/custom-call.0 | solution.py:19
  (136 shorter events, 36.2 us)
Async XLA Ops:
  7.2 2.2 copy-start
  7.2 285.2 %all-reduce.8.cloned.1.call-start = ((), (), s32[]{:S(2)}) async-start(), calls=%async_computation.1 | async-start | bytes 1048576 | tf_op jit(solution)/shard_map/psum | solution.py:35
  10.6 0.7 copy-start.7
  10.6 0.9 copy-start.1
  10.7 1.0 copy-start.6
  10.7 698.4 %all-reduce.6.cloned.1.call-start = ((), (), s32[]{:S(2)}) async-start(), calls=%async_computation | async-start | bytes 1048576 | tf_op jit(solution)/shard_map/psum | solution.py:58
  293.3 1.0 copy-start.4
  294.3 1.0 copy-start.5
  432.4 18.0 %collective-permute-start = (f32[128,256]{0,1:T(8,128)S(1)}, f32[128,256]{0,1:T(8,128)S(1)}, u32[]{:S(2)}, u32[]{:S(2)}) collective-permute-start(f32[128,256]{0,1:T(8,128)S(1)} %fusion.13), channel_id=1, source_target_pairs={{0,8},{8,16},{16,24},{24,32},{32,40},{40,48},{48,56},{56,64},{64,7... | collective-permute-start | bytes 393224 | tf_op jit(solution)/shard_map/ppermute | solution.py:15
  710.0 1.0 copy-start.3
  772.8 3.7 copy-start.2
  773.0 66.9 %collective-permute-start.1 = (f32[128,256]{0,1:T(8,128)S(1)}, f32[128,256]{0,1:T(8,128)S(1)}, u32[]{:S(2)}, u32[]{:S(2)}) collective-permute-start(f32[128,256]{0,1:T(8,128)S(1)} %fusion.14), channel_id=1, source_target_pairs={{0,8},{8,16},{16,24},{24,32},{32,40},{40,48},{48,56},{56,64},{64,7... | collective-permute-start | bytes 393224 | tf_op jit(solution)/shard_map/ppermute | solution.py:15
Sparse Core Ops, SparseCore 0:
  13.7 278.5 all-reduce.7
  437.1 271.9 all-reduce.5
where the time goes:
time: 859 us; the launch traced here: 848 us
  waiting for transfers between devices  550 us (64%)
  other arithmetic  231 us (27%)
  local copies, waits for them, and re-layouts  22 us (3%)
  between operations  20.4 us (2%)
  matrix products  16.8 us (2%)
    psum x2, waiting for transfers between devices, on_device(): lax.psum((cross_product(source, source), cross_product(target, target)),...  537 us
    another operation x9, other arithmetic, solve_right(): lax.linalg.triangular_solve(factor, gradient, left_side=False, lower=True...  90.1 us
    another operation x14, other arithmetic, on_device(): factor_source = jnp.linalg.cholesky(gram_source)  69.2 us
    another operation x14, other arithmetic, on_device(): factor_target = jnp.linalg.cholesky(gram_target)  69.2 us
  transfers between devices with their start and end apart: 4, of which 3 were waited for; matrix products, arithmetic and copies ran while one was open for 8% of the time, Pallas kernels for 0%

commit v1 on v0

v1 whole, which is shorter than its diff:
```python
import jax
import jax.numpy as jnp
from jax import lax
from jax.experimental import pallas as pl
from jax.experimental.pallas import tpu as pltpu
from jax.sharding import Mesh
from jax.sharding import PartitionSpec as P

step_size = 0.0002

AXES = ("xh", "xl", "ya", "yb", "yc", "zh", "zla", "zlb", "core")
WIDE = ("xh", "xl", "ya", "yb", "yc", "zh")
SCATTER = ("xh", "xl", "yc", "zlb", "core")
EXCHANGE = ("ya", "yb", "zh", "zla")
PIECES = 32
BLOCK = 32


def product(left, right, left_dim, right_dim):
    return lax.dot_general(
        left,
        right,
        (((left_dim,), (right_dim,)), ((), ())),
        precision=lax.Precision.HIGHEST,
        preferred_element_type=jnp.float32,
    )


def grid_of(shape):
    return lax.broadcasted_iota(jnp.int32, shape, 0), lax.broadcasted_iota(jnp.int32, shape, 1)


def sweep_panel(panel, first):
    rows, cols = panel.shape
    sub, lane = grid_of((8, cols))
    one_lane = lax.broadcasted_iota(jnp.int32, (1, cols), 1)
    groups = [panel[8 * g : 8 * g + 8] for g in range(rows // 8)]
    for row in range(rows):
        pivot, own = first + row, row // 8
        columns = [jnp.broadcast_to(g[:, pivot : pivot + 1], (8, cols)) for g in groups]
        scale = 1.0 / columns[own][row % 8 : row % 8 + 1]
        line = groups[own][row % 8 : row % 8 + 1]
        line = jnp.where(one_lane == pivot, scale, line * scale)
        full = jnp.broadcast_to(line, (8, cols))
        swept = []
        for g in range(rows // 8):
            value = jnp.where(lane == pivot, 0.0, groups[g]) - columns[g] * full
            swept.append(jnp.where(sub == row % 8, full, value) if g == own else value)
        groups = swept
    return jnp.concatenate(groups, 0)


def invert_pair(ref):
    size = ref.shape[1]
    half = size // 2

    def one_half(_, carry):
        lane = lax.broadcasted_iota(jnp.int32, (size, size), 1)
        for block in range(half // BLOCK):
            start = block * BLOCK
            for t in range(2):
                ref[t, start : start + BLOCK, :] = sweep_panel(ref[t, start : start + BLOCK, :], start)
            inside = (lane >= start) & (lane < start + BLOCK)
            for t in range(2):
                panel = ref[t, start : start + BLOCK, :]
                whole = ref[t]
                ref[t] = jnp.where(inside, 0.0, whole) - product(whole[:, start : start + BLOCK], panel, 1, 0)
                ref[t, start : start + BLOCK, :] = panel
        for t in range(2):
            whole = ref[t]
            ref[t, :half, :half] = whole[half:, half:]
            ref[t, :half, half:] = whole[half:, :half]
            ref[t, half:, :half] = whole[:half, half:]
            ref[t, half:, half:] = whole[:half, :half]
        return carry

    lax.fori_loop(0, 2, one_half, 0)


def gradients(source, target, observed, upper, lower):
    row = lax.broadcasted_iota(jnp.int32, observed.shape, 0)
    mask = jnp.where(row < observed.shape[0] // 2, upper, lower).astype(jnp.float32)
    residual = mask * (product(source, target, 1, 1) - observed)
    return product(residual, target, 1, 0), product(residual, source, 0, 0)


def diagonal(square):
    row, col = grid_of(square.shape)
    return jnp.sum(jnp.where(row == col, square, 0.0), axis=0, keepdims=True)


def first_kernel(tiles, source_ref, target_ref, observed_ref, grad_ref, moving_ref, sums_ref):
    source, target = source_ref[...], target_ref[...]
    count = target.shape[0]
    grad_source, grad_target = gradients(source, target, observed_ref[0], tiles[0, 0], tiles[0, 1])
    grad_ref[...] = grad_source
    moving_ref[:count, :] = target
    moving_ref[count:, :] = grad_target
    gram_source = product(source, source, 0, 0)
    gram_target = product(target, target, 0, 0)
    cross = product(source, grad_source, 0, 0)
    square_source = product(grad_source, grad_source, 0, 0)
    square_target = product(grad_target, grad_target, 0, 0)
    row, col = grid_of(cross.shape)
    upper = row <= col
    packed = (
        cross,
        jnp.where(upper, gram_source, gram_target),
        jnp.where(upper, square_source, square_target),
    )
    for place, square in enumerate(packed):
        for side in range(2):
            rows = slice(16 * place + 8 * side, 16 * place + 8 * side + 8)
            sums_ref[:, rows, :] = square[:, 128 * side : 128 * side + 128].reshape(PIECES, 8, 128)
    sums_ref[:, 48:56, :] = jnp.zeros((PIECES, 8, 128), jnp.float32)
    for place, square in enumerate((gram_target, square_target)):
        line = diagonal(square)
        for side in range(2):
            slot = 48 + 2 * place + side
            sums_ref[0, slot : slot + 1, :] = line[:, 128 * side : 128 * side + 128]


def unpacked(sums_ref, place):
    halves = [sums_ref[:, 16 * place + 8 * side : 16 * place + 8 * side + 8, :].reshape(256, 128) for side in range(2)]
    return jnp.concatenate(halves, 1)


def unpacked_pair(sums_ref, place):
    packed = unpacked(sums_ref, place)
    flipped = packed.T
    row, col = grid_of(packed.shape)
    line = jnp.concatenate([sums_ref[0, 46 + 2 * place + side : 47 + 2 * place + side, :] for side in range(2)], 1)
    first = jnp.where(row <= col, packed, flipped)
    second = jnp.where(row > col, packed, flipped)
    return first, jnp.where(row == col, line, second)


def updated_gram(gram, cross, square, inverse):
    moved = product(cross, inverse, 1, 0)
    twice = product(product(inverse, square, 1, 0), inverse, 1, 0)
    return gram - step_size * (moved + moved.T) + (step_size * step_size) * twice


def second_kernel(
    source_rows, target_rows,
    tiles, sums_ref, source_ref, grad_ref, moving_ref, observed_ref,
    source_out, grad_out, moving_out, gram_out, work,
):
    count = moving_ref.shape[0] // 2
    gram_source, gram_target = unpacked_pair(sums_ref, 1)
    work[0] = gram_source / source_rows
    work[1] = gram_target / target_rows
    invert_pair(work)
    source = source_ref[...] - step_size * product(grad_ref[...], work[1], 1, 0)
    target = moving_ref[:count, :] - step_size * product(moving_ref[count:, :], work[0], 1, 0)
    source_out[...] = source
    moving_out[:count, :] = target
    grad_source, grad_target = gradients(source, target, observed_ref[1], tiles[1, 0], tiles[1, 1])
    grad_out[...] = grad_source
    moving_out[count:, :] = grad_target
    gram_source, gram_target = unpacked_pair(sums_ref, 1)
    square_source, square_target = unpacked_pair(sums_ref, 2)
    cross = unpacked(sums_ref, 0)
    gram_out[0] = updated_gram(gram_source, cross, square_source, work[1]) / source_rows
    gram_out[1] = updated_gram(gram_target, cross.T, square_target, work[0]) / target_rows


def third_kernel(gram_ref, source_ref, grad_ref, source_out, inverse_out, work):
    work[...] = gram_ref[...]
    invert_pair(work)
    source_out[...] = source_ref[...] - step_size * product(grad_ref[...], work[1], 1, 0)
    inverse_out[...] = work[0]


def last_kernel(moving_ref, inverse_ref, target_out):
    count = moving_ref.shape[0] // 2
    target_out[...] = moving_ref[:count, :] - step_size * product(moving_ref[count:, :], inverse_ref[...], 1, 0)


def call(kernel, shapes, scratch, *arguments, scalars=0):
    vmem = pl.BlockSpec(memory_space=pltpu.VMEM)
    smem = pl.BlockSpec(memory_space=pltpu.SMEM)
    return pl.pallas_call(
        kernel,
        out_shape=[jax.ShapeDtypeStruct(shape, jnp.float32) for shape in shapes],
        in_specs=[smem] * scalars + [vmem] * (len(arguments) - scalars),
        out_specs=[vmem] * len(shapes),
        scratch_shapes=[pltpu.VMEM(shape, jnp.float32) for shape in scratch],
    )(*arguments)


def next_position(value):
    count = lax.axis_size(WIDE)
    return lax.ppermute(value, WIDE, [(place, (place + 1) % count) for place in range(count)])


def exchanged(value, axes):
    return lax.all_to_all(value, axes, 0, 0, tiled=True)


def spread(value, axes):
    return exchanged(jnp.broadcast_to(value[None], (lax.axis_size(axes), *value.shape)), axes)


def on_device(source, target, observed, tiles):
    devices = lax.axis_size(AXES)
    source_rows = source.shape[0] * devices
    target_rows = target.shape[0] * devices
    flags = tiles.reshape(2, 2)
    square = (256, 256)
    grad, moving, sums = call(
        first_kernel, (square, square, (PIECES, 56, 128)), (), flags, source, target, observed, scalars=1
    )
    moving = next_position(moving)
    sums = jnp.sum(exchanged(sums, SCATTER), axis=0)
    sums = jnp.sum(spread(sums, EXCHANGE), axis=0)
    sums = spread(sums, SCATTER)

    def middle(*refs):
        second_kernel(source_rows, target_rows, *refs)

    source, grad, moving, grams = call(
        middle, (square, square, square, (2, *square)), ((2, *square),),
        flags, sums, source, grad, moving, observed, scalars=1,
    )
    moving = next_position(moving)
    source, inverse = call(third_kernel, (square, square), ((2, *square),), grams, source, grad)
    (target,) = call(last_kernel, (target.shape,), (), moving, inverse)
    return source, target


def solution(mesh):
    fine = Mesh(mesh.devices.reshape((2,) * len(AXES)), AXES)
    placed = (P(AXES, None), P(AXES, None), P(None, AXES, None), P(None, AXES, None))
    return jax.shard_map(
        on_device, mesh=fine, in_specs=placed, out_specs=(P(AXES, None), P(AXES, None)), check_vma=False
    )
```

time: 859 us -> 161 us (0.19); the launches traced: 848 us -> 160 us
  waiting for transfers between devices: 550 us -> 20.3 us
  other arithmetic: 231 us -> 0.09 us
  Pallas kernels: 0 us -> 66.2 us
  blocking collectives: 0 us -> 56.9 us
  between operations: 20.4 us -> 0.68 us
  local copies, waits for them, and re-layouts: 22 us -> 2.76 us
  matrix products: 16.8 us -> 0 us
    psum x2 -> x0, waiting for transfers between devices: 537 us -> none  [on_device(): lax.psum((cross_product(source, source), cross_product(target, target)),...]
    another operation x37 -> x0, other arithmetic: 229 us -> none  [the longest x9 90.1 us: solve_right(): lax.linalg.triangular_solve(factor, gradient, left_side=False, lower=True...]
    pallas_call x0 -> x4, Pallas kernels: none -> 66.2 us  [call(): pl.pallas_call(kernel, out_shape=[jax.ShapeDtypeStruct(shape, jnp.float32...]
    all_to_all x0 -> x2, blocking collectives: none -> 56.9 us  [exchanged(): return lax.all_to_all(value, axes, 0, 0, tiled=True)]
    another operation x37 -> x0, local copies, waits for them, and re-layouts: 16.2 us -> none  [the longest x29 16.1 us: solve_right(): lax.linalg.triangular_solve(factor, gradient, left_side=False, lower=True...]
    another operation x32 -> x0, matrix products: 8.7 us -> none  [the longest x12 3.73 us: solve_right(): lax.linalg.triangular_solve(factor, gradient, left_side=False, lower=True...]
  transfers between devices with their start and end apart: 4 -> 3, of which waited for: 3 -> 1; matrix products, arithmetic and copies ran while one was open for 8% -> 0% of each run, Pallas kernels for 0% -> 18%
where the time goes in v1:
time: 161 us; the launch traced here: 160 us
  Pallas kernels  66.2 us (41%)
  blocking collectives  56.9 us (35%)
  waiting for transfers between devices  20.3 us (13%)
  starting transfers between devices  13.2 us (8%)
  local copies, waits for them, and re-layouts  2.76 us (2%)
    pallas_call x4, Pallas kernels, call(): pl.pallas_call(kernel, out_shape=[jax.ShapeDtypeStruct(shape, jnp.float32...  66.2 us
    all_to_all x2, blocking collectives, exchanged(): return lax.all_to_all(value, axes, 0, 0, tiled=True)  56.9 us
    ppermute x2, waiting for transfers between devices, next_position(): lax.ppermute(value, WIDE, [(place, (place + 1) % count) for place in rang...  20.3 us
    ppermute x2, starting transfers between devices, next_position(): lax.ppermute(value, WIDE, [(place, (place + 1) % count) for place in rang...  9.12 us
    all_to_all x1, starting transfers between devices, exchanged(): return lax.all_to_all(value, axes, 0, 0, tiled=True)  4.1 us
  transfers between devices with their start and end apart: 3, of which 1 were waited for; matrix products, arithmetic and copies ran while one was open for 0% of the time, Pallas kernels for 18%

profile of v1, /device:TPU:1, one launch (start us, length us, event | category | flops | bytes accessed | tf_op | source)
XLA Modules:
  0.0 160.2 jit_solution(15757333263894988283)
XLA Ops:
  0.6 4.0 %shard_map.59 = (f32[256,256]{1,0:T(8,128)}, f32[256,256]{1,0:T(8,128)}, f32[32,56,128]{2,1,0:T(8,128)}) custom-call(s32[2,2]{1,0:T(2,128)} %bitcast.1, f32[256,256]{1,0:T(8,128)} %refs_2_.1, f32[128,256]{1,0:T(8,128)} %target_ref.1, f32[2,256,128]{2,1,0:T(8,128)} %refs_5_.1), custom_call_target="tpu_custom_call" | custom-call | tf_op jit(solution)/shard_map/pallas_call | solution.py:183
  4.6 25.8 %all_to_all.15 = f32[32,56,128]{2,1,0:T(8,128)S(1)} all-to-all(f32[32,56,128]{2,1,0:T(8,128)} %get-tuple-element.11), channel_id=1, replica_groups=mesh['xh'=2,'xl'=2,'ya'=2,'yb'=2,'yc'=2,'zh'=2,'zla'=2,'zlb'=2,'core'=2]..., dimensions={0} | all-to-all | bytes 1835008 | tf_op jit(solution)/shard_map/all_to_all | solution.py:198
  30.5 0.1 reduce_sum.18
  30.6 31.1 %all_to_all.16 = f32[16,56,128]{2,1,0:T(8,128)S(1)} all-to-all(f32[16,56,128]{2,1,0:T(8,128)S(1)} %broadcast_in_dim.4), channel_id=1, replica_groups=mesh['xh'=2,'xl'=2,'ya'=2,'yb'=2,'yc'=2,'zh'=2,'zla'=2,'zlb'=2,'core'=2]..., dimensions={0} | all-to-all | bytes 917504 | tf_op jit(solution)/shard_map/all_to_all | solution.py:198
  61.7 1.0 broadcast_in_dim.5
  62.7 0.0 copy-start.3
  62.7 4.1 %all-to-all-start.2 = ((f32[32,56,128]{2,1,0:T(8,128)}), f32[32,56,128]{2,1,0:T(8,128)S(1)}, u32[]{:S(2)}, u32[]{:S(2)}) async-start(f32[32,56,128]{2,1,0:T(8,128)} %broadcast_in_dim.5), calls=%async_computation.2 | async-start | bytes 1835008 | tf_op jit(solution)/shard_map/all_to_all | solution.py:198
  66.8 0.0 copy-done.3
  66.8 2.8 %collective-permute-start = (f32[256,256]{1,0:T(8,128)S(1)}, f32[256,256]{1,0:T(8,128)S(1)}, u32[]{:S(2)}, u32[]{:S(2)}) collective-permute-start(f32[256,256]{1,0:T(8,128)S(1)} %copy-done.3), channel_id=1, source_target_pairs={{0,8},{8,16},{16,24},{24,32},{32,40},{40,48},{48,56},{56,64},{64,7... | collective-permute-start | bytes 786440 | tf_op jit(solution)/shard_map/ppermute | solution.py:194
  69.6 20.3 %collective-permute-done.refs_4_ = f32[256,256]{1,0:T(8,128)S(1)} collective-permute-done((f32[256,256]{1,0:T(8,128)S(1)}, f32[256,256]{1,0:T(8,128)S(1)}, u32[]{:S(2)}, u32[]{:S(2)}) %collective-permute-start) | collective-permute-done | bytes 262176 | tf_op jit(solution)/shard_map/ppermute | solution.py:194
  90.0 0.0 copy-start.1
  90.0 0.0 all-to-all-done.2.refs_1_
  90.0 0.0 copy-start
  90.0 0.7 copy-done.1
  90.7 0.3 copy-done
  91.0 31.8 %shard_map.60 = (f32[256,256]{1,0:T(8,128)}, f32[256,256]{1,0:T(8,128)}, f32[256,256]{1,0:T(8,128)}, f32[2,256,256]{2,1,0:T(8,128)}) custom-call(s32[2,2]{1,0:T(2,128)} %bitcast.2, f32[32,56,128]{2,1,0:T(8,128)} %copy-done, f32[256,256]{1,0:T(8,128)} %refs_2_.1, f32[256,256]{1,0:T(8,128)} %get-tuple-element.12.refs_3_, f32[256,256]{1,0:T(8,128)} %copy-done.1, ...), custom_call_target="tpu_custom_call" | custom-call | tf_op jit(solution)/shard_map/pallas_call | solution.py:183
  122.8 6.3 %collective-permute-start.1 = (f32[256,256]{1,0:T(8,128)}, f32[256,256]{1,0:T(8,128)S(1)}, u32[]{:S(2)}, u32[]{:S(2)}) collective-permute-start(f32[256,256]{1,0:T(8,128)} %get-tuple-element.18), channel_id=1, source_target_pairs={{0,8},{8,16},{16,24},{24,32},{32,40},{40,48},{48,56},{56,64},{64,7... | collective-permute-start | bytes 786440 | tf_op jit(solution)/shard_map/ppermute | solution.py:194
  129.1 28.4 %shard_map.61 = (f32[256,256]{1,0:T(8,128)}, f32[256,256]{1,0:T(8,128)}) custom-call(f32[2,256,256]{2,1,0:T(8,128)} %get-tuple-element.14.gram_ref, f32[256,256]{1,0:T(8,128)} %get-tuple-element.15.source_ref, f32[256,256]{1,0:T(8,128)} %get-tuple-element.16.grad_ref), custom_call_target="tpu_custom_call" | custom-call | tf_op jit(solution)/shard_map/pallas_call | solution.py:183
  157.6 0.0 collective-permute-done.1.moving_ref
  157.6 0.0 copy-start.2
  157.6 0.7 copy-done.2
  158.3 2.0 %shard_map.62 = f32[128,256]{1,0:T(8,128)} custom-call(f32[256,256]{1,0:T(8,128)} %copy-done.2, f32[256,256]{1,0:T(8,128)} %get-tuple-element.19.inverse_ref), custom_call_target="tpu_custom_call" | custom-call | tf_op jit(solution)/shard_map/pallas_call | solution.py:183
  (2 shorter events, 0.1 us)
Async XLA Ops:
  62.7 4.1 %copy-start.3 = (f32[256,256]{1,0:T(8,128)S(1)}, f32[256,256]{1,0:T(8,128)}, u32[]{:S(2)}) copy-start(f32[256,256]{1,0:T(8,128)} %get-tuple-element.13) | copy-start | bytes 786436
  62.7 27.3 %all-to-all-start.2 = ((f32[32,56,128]{2,1,0:T(8,128)}), f32[32,56,128]{2,1,0:T(8,128)S(1)}, u32[]{:S(2)}, u32[]{:S(2)}) async-start(f32[32,56,128]{2,1,0:T(8,128)} %broadcast_in_dim.5), calls=%async_computation.2 | async-start | bytes 1835008 | tf_op jit(solution)/shard_map/all_to_all | solution.py:198
  66.8 23.1 %collective-permute-start = (f32[256,256]{1,0:T(8,128)S(1)}, f32[256,256]{1,0:T(8,128)S(1)}, u32[]{:S(2)}, u32[]{:S(2)}) collective-permute-start(f32[256,256]{1,0:T(8,128)S(1)} %copy-done.3), channel_id=1, source_target_pairs={{0,8},{8,16},{16,24},{24,32},{32,40},{40,48},{48,56},{56,64},{64,7... | collective-permute-start | bytes 786440 | tf_op jit(solution)/shard_map/ppermute | solution.py:194
  90.0 0.7 copy-start.1
  90.0 1.0 copy-start
  122.8 34.8 %collective-permute-start.1 = (f32[256,256]{1,0:T(8,128)}, f32[256,256]{1,0:T(8,128)S(1)}, u32[]{:S(2)}, u32[]{:S(2)}) collective-permute-start(f32[256,256]{1,0:T(8,128)} %get-tuple-element.18), channel_id=1, source_target_pairs={{0,8},{8,16},{16,24},{24,32},{32,40},{40,48},{48,56},{56,64},{64,7... | collective-permute-start | bytes 786440 | tf_op jit(solution)/shard_map/ppermute | solution.py:194
  157.6 0.7 copy-start.2

commit v2 on v1

--- a/solution.py
+++ b/solution.py
@@ -13,7 +13,7 @@
 SCATTER = ("xh", "xl", "yc", "zlb", "core")
 EXCHANGE = ("ya", "yb", "zh", "zla")
 PIECES = 32
-BLOCK = 32
+BLOCK = 64
 
 
 def product(left, right, left_dim, right_dim):
@@ -30,51 +30,91 @@
     return lax.broadcasted_iota(jnp.int32, shape, 0), lax.broadcasted_iota(jnp.int32, shape, 1)
 
 
-def sweep_panel(panel, first):
-    rows, cols = panel.shape
+def sweep_pair(panels, first):
+    rows, cols = panels[0].shape
     sub, lane = grid_of((8, cols))
-    one_lane = lax.broadcasted_iota(jnp.int32, (1, cols), 1)
-    groups = [panel[8 * g : 8 * g + 8] for g in range(rows // 8)]
-    for row in range(rows):
-        pivot, own = first + row, row // 8
-        columns = [jnp.broadcast_to(g[:, pivot : pivot + 1], (8, cols)) for g in groups]
-        scale = 1.0 / columns[own][row % 8 : row % 8 + 1]
-        line = groups[own][row % 8 : row % 8 + 1]
-        line = jnp.where(one_lane == pivot, scale, line * scale)
-        full = jnp.broadcast_to(line, (8, cols))
-        swept = []
-        for g in range(rows // 8):
-            value = jnp.where(lane == pivot, 0.0, groups[g]) - columns[g] * full
-            swept.append(jnp.where(sub == row % 8, full, value) if g == own else value)
-        groups = swept
-    return jnp.concatenate(groups, 0)
+    if first:
+        panels = [pltpu.roll(panel, cols - first, 1) for panel in panels]
+    start = tuple(tuple(panel[8 * g : 8 * g + 8] for g in range(rows // 8)) for panel in panels)
+
+    def wide(value):
+        return jnp.broadcast_to(value, (8, cols))
+
+    def eight_pivots(_, carry):
+        held = [list(groups) for groups in carry]
+        for r in range(0, 8, 2):
+            here, after = lane == r, lane == r + 1
+            for t, groups in enumerate(held):
+                left = [wide(group[:, r : r + 1]) for group in groups]
+                right = [wide(group[:, r + 1 : r + 2]) for group in groups]
+                upper = jnp.where(after, 0.0, jnp.where(here, 1.0, wide(groups[0][r : r + 1])))
+                lower = jnp.where(here, 0.0, jnp.where(after, 1.0, wide(groups[0][r + 1 : r + 2])))
+                main = jnp.where(sub == r, left[0], right[0])
+                cross = wide(jnp.where(sub == r, right[0], left[0])[r : r + 1])
+                first_pivot, second_pivot = wide(main[r : r + 1]), wide(main[r + 1 : r + 2])
+                scale = 1.0 / (first_pivot * second_pivot - cross * cross)
+                upper, lower = (
+                    scale * (second_pivot * upper - cross * lower),
+                    scale * (first_pivot * lower - cross * upper),
+                )
+                swept = [
+                    jnp.where(here | after, 0.0, group) - left[g] * upper - right[g] * lower
+                    for g, group in enumerate(groups)
+                ]
+                swept[0] = jnp.where(sub == r, upper, jnp.where(sub == r + 1, lower, swept[0]))
+                held[t] = swept
+        return tuple(tuple(pltpu.roll(group, cols - 8, 1) for group in groups[1:] + groups[:1]) for groups in held)
+
+    swept = [jnp.concatenate(groups, 0) for groups in lax.fori_loop(0, rows // 8, eight_pivots, start)]
+    back = (first + rows) % cols
+    return [pltpu.roll(panel, back, 1) for panel in swept] if back else swept
+
+
+def invert_blocks(squares):
+    size = squares[0].shape[0]
+    lane = lax.broadcasted_iota(jnp.int32, (BLOCK, size), 1)
+    panels = [[square[start : start + BLOCK] for start in range(0, size, BLOCK)] for square in squares]
+    for block in range(size // BLOCK):
+        start = block * BLOCK
+        swept = sweep_pair([held[block] for held in panels], start)
+        inside = (lane >= start) & (lane < start + BLOCK)
+        for held, panel in zip(panels, swept):
+            for other in range(len(held)):
+                left = held[other][:, start : start + BLOCK]
+                if other != block:
+                    held[other] = jnp.where(inside, 0.0, held[other]) - product(left, panel, 1, 0)
+            held[block] = panel
+    return [jnp.concatenate(held, 0) for held in panels]
 
 
 def invert_pair(ref):
     size = ref.shape[1]
     half = size // 2
-
-    def one_half(_, carry):
-        lane = lax.broadcasted_iota(jnp.int32, (size, size), 1)
-        for block in range(half // BLOCK):
-            start = block * BLOCK
-            for t in range(2):
-                ref[t, start : start + BLOCK, :] = sweep_panel(ref[t, start : start + BLOCK, :], start)
-            inside = (lane >= start) & (lane < start + BLOCK)
-            for t in range(2):
-                panel = ref[t, start : start + BLOCK, :]
-                whole = ref[t]
-                ref[t] = jnp.where(inside, 0.0, whole) - product(whole[:, start : start + BLOCK], panel, 1, 0)
-                ref[t, start : start + BLOCK, :] = panel
-        for t in range(2):
-            whole = ref[t]
-            ref[t, :half, :half] = whole[half:, half:]
-            ref[t, :half, half:] = whole[half:, :half]
-            ref[t, half:, :half] = whole[:half, half:]
-            ref[t, half:, half:] = whole[:half, :half]
-        return carry
-
-    lax.fori_loop(0, 2, one_half, 0)
+    row, col = grid_of((size, size))
+    scales = []
+    for t in range(2):
+        whole = ref[t]
+        main = jnp.where(row == col, whole, 0.0)
+        across = lax.rsqrt(jnp.sum(main, axis=0, keepdims=True))
+        down = lax.rsqrt(jnp.sum(main, axis=1, keepdims=True))
+        scales.append((across, down))
+        ref[t] = whole * across * down
+    leading = invert_blocks([ref[t, :half, :half] for t in range(2)])
+    ratio = [product(leading[t], ref[t, :half, half:], 1, 0) for t in range(2)]
+    rest = [ref[t, half:, half:] - product(ref[t, :half, half:], ratio[t], 0, 0) for t in range(2)]
+    for t in range(2):
+        ref[t, :half, :half] = leading[t]
+        ref[t, :half, half:] = ratio[t]
+    trailing = invert_blocks(rest)
+    for t in range(2):
+        across, down = scales[t]
+        ratio = ref[t, :half, half:]
+        corner = -product(ratio, trailing[t], 1, 0)
+        top = ref[t, :half, :half] - product(corner, ratio, 1, 1)
+        ref[t, :half, :half] = top * across[:, :half] * down[:half]
+        ref[t, :half, half:] = corner * across[:, half:] * down[:half]
+        ref[t, half:, :half] = corner.T * across[:, :half] * down[half:]
+        ref[t, half:, half:] = trailing[t] * across[:, half:] * down[half:]
 
 
 def gradients(source, target, observed, upper, lower):
@@ -141,28 +181,30 @@
     return gram - step_size * (moved + moved.T) + (step_size * step_size) * twice
 
 
+def inverse_kernel(source_rows, target_rows, sums_ref, gram_out, inverse_out):
+    gram_out[0], gram_out[1] = unpacked_pair(sums_ref, 1)
+    inverse_out[0] = gram_out[0] / source_rows
+    inverse_out[1] = gram_out[1] / target_rows
+    invert_pair(inverse_out)
+
+
 def second_kernel(
     source_rows, target_rows,
-    tiles, sums_ref, source_ref, grad_ref, moving_ref, observed_ref,
-    source_out, grad_out, moving_out, gram_out, work,
+    tiles, sums_ref, gram_ref, inverse_ref, source_ref, grad_ref, moving_ref, observed_ref,
+    source_out, grad_out, moving_out, gram_out,
 ):
     count = moving_ref.shape[0] // 2
-    gram_source, gram_target = unpacked_pair(sums_ref, 1)
-    work[0] = gram_source / source_rows
-    work[1] = gram_target / target_rows
-    invert_pair(work)
-    source = source_ref[...] - step_size * product(grad_ref[...], work[1], 1, 0)
-    target = moving_ref[:count, :] - step_size * product(moving_ref[count:, :], work[0], 1, 0)
+    source = source_ref[...] - step_size * product(grad_ref[...], inverse_ref[1], 1, 0)
+    target = moving_ref[:count, :] - step_size * product(moving_ref[count:, :], inverse_ref[0], 1, 0)
     source_out[...] = source
     moving_out[:count, :] = target
     grad_source, grad_target = gradients(source, target, observed_ref[1], tiles[1, 0], tiles[1, 1])
     grad_out[...] = grad_source
     moving_out[count:, :] = grad_target
-    gram_source, gram_target = unpacked_pair(sums_ref, 1)
     square_source, square_target = unpacked_pair(sums_ref, 2)
     cross = unpacked(sums_ref, 0)
-    gram_out[0] = updated_gram(gram_source, cross, square_source, work[1]) / source_rows
-    gram_out[1] = updated_gram(gram_target, cross.T, square_target, work[0]) / target_rows
+    gram_out[0] = updated_gram(gram_ref[0], cross, square_source, inverse_ref[1]) / source_rows
+    gram_out[1] = updated_gram(gram_ref[1], cross.T, square_target, inverse_ref[0]) / target_rows
 
 
 def third_kernel(gram_ref, source_ref, grad_ref, source_out, inverse_out, work):
@@ -170,11 +212,6 @@
     invert_pair(work)
     source_out[...] = source_ref[...] - step_size * product(grad_ref[...], work[1], 1, 0)
     inverse_out[...] = work[0]
-
-
-def last_kernel(moving_ref, inverse_ref, target_out):
-    count = moving_ref.shape[0] // 2
-    target_out[...] = moving_ref[:count, :] - step_size * product(moving_ref[count:, :], inverse_ref[...], 1, 0)
 
 
 def call(kernel, shapes, scratch, *arguments, scalars=0):
@@ -211,21 +248,27 @@
     grad, moving, sums = call(
         first_kernel, (square, square, (PIECES, 56, 128)), (), flags, source, target, observed, scalars=1
     )
-    moving = next_position(moving)
     sums = jnp.sum(exchanged(sums, SCATTER), axis=0)
     sums = jnp.sum(spread(sums, EXCHANGE), axis=0)
-    sums = spread(sums, SCATTER)
+    sums, moving = lax.optimization_barrier((spread(sums, SCATTER), moving))
+    moving = next_position(moving)
+
+    def inverses(*refs):
+        inverse_kernel(source_rows, target_rows, *refs)
 
     def middle(*refs):
         second_kernel(source_rows, target_rows, *refs)
 
+    pair = (2, *square)
+    grams, inverse = call(inverses, (pair, pair), (), sums)
     source, grad, moving, grams = call(
-        middle, (square, square, square, (2, *square)), ((2, *square),),
-        flags, sums, source, grad, moving, observed, scalars=1,
+        middle, (square, square, square, pair), (),
+        flags, sums, grams, inverse, source, grad, moving, observed, scalars=1,
     )
     moving = next_position(moving)
     source, inverse = call(third_kernel, (square, square), ((2, *square),), grams, source, grad)
-    (target,) = call(last_kernel, (target.shape,), (), moving, inverse)
+    count = target.shape[0]
+    target = moving[:count] - step_size * product(moving[count:], inverse, 1, 0)
     return source, target
 
 

time: 161 us -> 138 us (0.86)
  waiting for transfers between devices: 20.3 us -> 0.01 us
  blocking collectives: 56.9 us -> 76.2 us
  Pallas kernels: 66.2 us -> 49.8 us
  starting transfers between devices: 13.2 us -> 8.53 us
  local copies, waits for them, and re-layouts: 2.76 us -> 0.8 us
  matrix products: 0 us -> 1.89 us
    ppermute x2, waiting for transfers between devices: 20.3 us -> 0.01 us  [next_position(): lax.ppermute(value, WIDE, [(place, (place + 1) % count) for place in rang...]
    all_to_all x2 -> x3, blocking collectives: 56.9 us -> 76.2 us  [exchanged(): return lax.all_to_all(value, axes, 0, 0, tiled=True)]
    pallas_call x4, Pallas kernels: 66.2 us -> 49.8 us  [call(): pl.pallas_call(kernel, out_shape=[jax.ShapeDtypeStruct(shape, jnp.float32...]
    all_to_all x1 -> x0, starting transfers between devices: 4.1 us -> none  [exchanged(): return lax.all_to_all(value, axes, 0, 0, tiled=True)]
    dot_general x0 -> x1, matrix products: none -> 1.89 us  [product(): lax.dot_general(left, right, (((left_dim,), (right_dim,)), ((), ())), pre...]
  transfers between devices with their start and end apart: 3 -> 2, of which waited for: 1 -> 0; matrix products, arithmetic and copies ran while one was open for 0% -> 0% of each run, Pallas kernels for 18% -> 29%
where the time goes in v2:
time: 138 us
  blocking collectives  76.2 us (55%)
  Pallas kernels  49.8 us (36%)
  starting transfers between devices  8.53 us (6%)
  matrix products  1.89 us (1%)
    all_to_all x3, blocking collectives, exchanged(): return lax.all_to_all(value, axes, 0, 0, tiled=True)  76.2 us
    pallas_call x4, Pallas kernels, call(): pl.pallas_call(kernel, out_shape=[jax.ShapeDtypeStruct(shape, jnp.float32...  49.8 us
    ppermute x2, starting transfers between devices, next_position(): lax.ppermute(value, WIDE, [(place, (place + 1) % count) for place in rang...  8.53 us
  transfers between devices with their start and end apart: 2, of which 0 were waited for; matrix products, arithmetic and copies ran while one was open for 0% of the time, Pallas kernels for 29%

profile of v2, /device:TPU:1, one launch (start us, length us, event | category | flops | bytes accessed | tf_op | source)
XLA Modules:
  0.0 138.0 jit_solution(2172335907817485343)
XLA Ops:
  0.6 4.0 %shard_map.59 = (f32[256,256]{1,0:T(8,128)}, f32[256,256]{1,0:T(8,128)}, f32[32,56,128]{2,1,0:T(8,128)}) custom-call(s32[2,2]{1,0:T(2,128)} %bitcast.2, f32[256,256]{1,0:T(8,128)} %refs_4_.1, f32[128,256]{1,0:T(8,128)} %target_ref.1, f32[2,256,128]{2,1,0:T(8,128)} %refs_7_.1), custom_call_target="tpu_custom_call" | custom-call | tf_op jit(solution)/shard_map/pallas_call | solution.py:220
  4.6 25.8 %all_to_all.15 = f32[32,56,128]{2,1,0:T(8,128)S(1)} all-to-all(f32[32,56,128]{2,1,0:T(8,128)} %get-tuple-element.15), channel_id=1, replica_groups=mesh['xh'=2,'xl'=2,'ya'=2,'yb'=2,'yc'=2,'zh'=2,'zla'=2,'zlb'=2,'core'=2]..., dimensions={0} | all-to-all | bytes 1835008 | tf_op jit(solution)/shard_map/all_to_all | solution.py:235
  30.4 0.1 reduce_sum.18
  30.5 31.1 %all_to_all.16 = f32[16,56,128]{2,1,0:T(8,128)S(1)} all-to-all(f32[16,56,128]{2,1,0:T(8,128)S(1)} %broadcast_in_dim.4), channel_id=1, replica_groups=mesh['xh'=2,'xl'=2,'ya'=2,'yb'=2,'yc'=2,'zh'=2,'zla'=2,'zlb'=2,'core'=2]..., dimensions={0} | all-to-all | bytes 917504 | tf_op jit(solution)/shard_map/all_to_all | solution.py:235
  61.7 0.1 broadcast_in_dim.5
  61.8 0.0 copy-start.1
  61.8 19.3 %all_to_all.17.refs_0_.refs_1_ = f32[32,56,128]{2,1,0:T(8,128)} all-to-all(f32[32,56,128]{2,1,0:T(8,128)S(1)} %broadcast_in_dim.5), channel_id=1, replica_groups=mesh['xh'=2,'xl'=2,'ya'=2,'yb'=2,'yc'=2,'zh'=2,'zla'=2,'zlb'=2,'core'=2]..., dimensions={0} | all-to-all | bytes 1835008 | tf_op jit(solution)/shard_map/all_to_all | solution.py:235
  81.1 0.0 copy-done.1
  81.1 2.8 %collective-permute-start = (f32[256,256]{1,0:T(8,128)S(1)}, f32[256,256]{1,0:T(8,128)S(1)}, u32[]{:S(2)}, u32[]{:S(2)}) collective-permute-start(f32[256,256]{1,0:T(8,128)S(1)} %copy-done.1), channel_id=1, source_target_pairs={{0,8},{8,16},{16,24},{24,32},{32,40},{40,48},{48,56},{56,64},{64,7... | collective-permute-start | bytes 786440 | tf_op jit(solution)/shard_map/ppermute | solution.py:231
  83.9 19.7 %shard_map.60 = (f32[2,256,256]{2,1,0:T(8,128)}, f32[2,256,256]{2,1,0:T(8,128)}) custom-call(f32[32,56,128]{2,1,0:T(8,128)} %all_to_all.17.refs_0_.refs_1_), custom_call_target="tpu_custom_call" | custom-call | tf_op jit(solution)/shard_map/pallas_call | solution.py:220
  103.6 0.0 collective-permute-done.refs_6_
  103.7 0.0 copy-start
  103.7 0.7 copy-done
  104.4 5.9 %shard_map.61 = (f32[256,256]{1,0:T(8,128)}, f32[256,256]{1,0:T(8,128)}, f32[256,256]{1,0:T(8,128)}, f32[2,256,256]{2,1,0:T(8,128)}) custom-call(s32[2,2]{1,0:T(2,128)} %bitcast.3, f32[32,56,128]{2,1,0:T(8,128)} %all_to_all.17.refs_0_.refs_1_, f32[2,256,256]{2,1,0:T(8,128)} %get-tuple-element.18.refs_2_, f32[2,256,256]{2,1,0:T(8,128)} %get-tuple-element.19.refs_3_, ...), custom_call_target="tpu_custom_call" | custom-call | tf_op jit(solution)/shard_map/pallas_call | solution.py:220
  110.2 5.7 %collective-permute-start.1 = (f32[256,256]{1,0:T(8,128)}, f32[256,256]{1,0:T(8,128)S(1)}, u32[]{:S(2)}, u32[]{:S(2)}) collective-permute-start(f32[256,256]{1,0:T(8,128)} %get-tuple-element.26), channel_id=1, source_target_pairs={{0,8},{8,16},{16,24},{24,32},{32,40},{40,48},{48,56},{56,64},{64,7... | collective-permute-start | bytes 786440 | tf_op jit(solution)/shard_map/ppermute | solution.py:231
  115.9 20.1 %shard_map.62 = (f32[256,256]{1,0:T(8,128)}, f32[256,256]{1,0:T(8,128)}) custom-call(f32[2,256,256]{2,1,0:T(8,128)} %get-tuple-element.22.gram_ref, f32[256,256]{1,0:T(8,128)} %get-tuple-element.23.source_ref, f32[256,256]{1,0:T(8,128)} %get-tuple-element.24.grad_ref), custom_call_target="tpu_custom_call" | custom-call | tf_op jit(solution)/shard_map/pallas_call | solution.py:220
  136.1 0.0 collective-permute-done.1
  136.1 1.9 %slice_subtract_fusion = f32[128,256]{1,0:T(8,128)} fusion(f32[256,256]{1,0:T(8,128)S(1)} %collective-permute-done.1, f32[256,256]{1,0:T(8,128)} %get-tuple-element.27), kind=kOutput, calls=%fused_computation.2 | convolution fusion | flops 100728832 | bytes 655360 | tf_op jit(solution)/shard_map/dot_general | solution.py:20
  (2 shorter events, 0.1 us)
Async XLA Ops:
  61.8 19.3 %copy-start.1 = (f32[256,256]{1,0:T(8,128)S(1)}, f32[256,256]{1,0:T(8,128)}, u32[]{:S(2)}) copy-start(f32[256,256]{1,0:T(8,128)} %get-tuple-element.21) | copy-start | bytes 786436
  81.1 22.6 %collective-permute-start = (f32[256,256]{1,0:T(8,128)S(1)}, f32[256,256]{1,0:T(8,128)S(1)}, u32[]{:S(2)}, u32[]{:S(2)}) collective-permute-start(f32[256,256]{1,0:T(8,128)S(1)} %copy-done.1), channel_id=1, source_target_pairs={{0,8},{8,16},{16,24},{24,32},{32,40},{40,48},{48,56},{56,64},{64,7... | collective-permute-start | bytes 786440 | tf_op jit(solution)/shard_map/ppermute | solution.py:231
  103.7 0.7 copy-start
  110.2 25.9 %collective-permute-start.1 = (f32[256,256]{1,0:T(8,128)}, f32[256,256]{1,0:T(8,128)S(1)}, u32[]{:S(2)}, u32[]{:S(2)}) collective-permute-start(f32[256,256]{1,0:T(8,128)} %get-tuple-element.26), channel_id=1, source_target_pairs={{0,8},{8,16},{16,24},{24,32},{32,40},{40,48},{48,56},{56,64},{64,7... | collective-permute-start | bytes 786440 | tf_op jit(solution)/shard_map/ppermute | solution.py:231

commit v3 on v2

--- a/solution.py
+++ b/solution.py
@@ -10,8 +10,8 @@
 
 AXES = ("xh", "xl", "ya", "yb", "yc", "zh", "zla", "zlb", "core")
 WIDE = ("xh", "xl", "ya", "yb", "yc", "zh")
-SCATTER = ("xh", "xl", "yc", "zlb", "core")
-EXCHANGE = ("ya", "yb", "zh", "zla")
+NEAR = ("xh", "xl", "yc", "zlb")
+FAR = (("ya", "yb"), ("zh", "zla"))
 PIECES = 32
 BLOCK = 64
 
@@ -248,9 +248,13 @@
     grad, moving, sums = call(
         first_kernel, (square, square, (PIECES, 56, 128)), (), flags, source, target, observed, scalars=1
     )
-    sums = jnp.sum(exchanged(sums, SCATTER), axis=0)
-    sums = jnp.sum(spread(sums, EXCHANGE), axis=0)
-    sums, moving = lax.optimization_barrier((spread(sums, SCATTER), moving))
+    shape = sums.shape
+    sums = jnp.sum(exchanged(sums.reshape(2, -1, 128), "core"), axis=0)
+    sums = jnp.sum(exchanged(sums.reshape(-1, *shape[1:]), NEAR), axis=0)
+    for axes in FAR:
+        sums = jnp.sum(spread(sums, axes), axis=0)
+    sums = spread(sums, NEAR).reshape(-1, 128)
+    sums, moving = lax.optimization_barrier((spread(sums, "core").reshape(shape), moving))
     moving = next_position(moving)
 
     def inverses(*refs):

time: 138 us -> 137 us (level)
  blocking collectives: 76.2 us -> 73.4 us
    all_to_all x3 -> x6, blocking collectives: 76.2 us -> 73.4 us  [exchanged(): return lax.all_to_all(value, axes, 0, 0, tiled=True)]
where the time goes in v3:
time: 137 us; the launch traced here: 136 us
  blocking collectives  73.4 us (54%)
  Pallas kernels  49.8 us (36%)
  starting transfers between devices  9.29 us (7%)
  matrix products  1.89 us (1%)
    all_to_all x6, blocking collectives, exchanged(): return lax.all_to_all(value, axes, 0, 0, tiled=True)  73.4 us
    pallas_call x4, Pallas kernels, call(): pl.pallas_call(kernel, out_shape=[jax.ShapeDtypeStruct(shape, jnp.float32...  49.8 us
    ppermute x2, starting transfers between devices, next_position(): lax.ppermute(value, WIDE, [(place, (place + 1) % count) for place in rang...  9.29 us
  transfers between devices with their start and end apart: 2, of which 0 were waited for; matrix products, arithmetic and copies ran while one was open for 0% of the time, Pallas kernels for 29%

profile of v3, /device:TPU:1, one launch (start us, length us, event | category | flops | bytes accessed | tf_op | source)
XLA Modules:
  0.0 136.0 jit_solution(17978775176749018829)
XLA Ops:
  0.6 4.0 %shard_map.59 = (f32[256,256]{1,0:T(8,128)}, f32[256,256]{1,0:T(8,128)}, f32[32,56,128]{2,1,0:T(8,128)}) custom-call(s32[2,2]{1,0:T(2,128)} %bitcast.11, f32[256,256]{1,0:T(8,128)} %refs_4_.1, f32[128,256]{1,0:T(8,128)} %target_ref.1, f32[2,256,128]{2,1,0:T(8,128)} %refs_7_.1), custom_call_target="tpu_custom_call" | custom-call | tf_op jit(solution)/shard_map/pallas_call | solution.py:220
  4.6 12.0 %all_to_all.30 = f32[2,896,128]{2,1,0:T(8,128)S(1)} all-to-all(f32[2,896,128]{2,1,0:T(8,128)} %bitcast.10), channel_id=1, replica_groups=mesh['xh'=2,'xl'=2,'ya'=2,'yb'=2,'yc'=2,'zh'=2,'zla'=2,'zlb'=2,'core'=2]..., dimensions={0} | all-to-all | bytes 1835008 | tf_op jit(solution)/shard_map/all_to_all | solution.py:235
  16.6 0.1 reduce_sum.36
  16.7 11.6 %all_to_all.31 = f32[16,56,128]{2,1,0:T(8,128)S(1)} all-to-all(f32[16,56,128]{2,1,0:T(8,128)S(1)} %bitcast.8), channel_id=1, replica_groups=mesh['xh'=2,'xl'=2,'ya'=2,'yb'=2,'yc'=2,'zh'=2,'zla'=2,'zlb'=2,'core'=2]..., dimensions={0} | all-to-all | bytes 917504 | tf_op jit(solution)/shard_map/all_to_all | solution.py:235
  28.4 11.2 %all_to_all.32 = f32[4,56,128]{2,1,0:T(8,128)S(1)} all-to-all(f32[4,56,128]{2,1,0:T(8,128)S(1)} %broadcast_in_dim.10), channel_id=1, replica_groups=mesh['xh'=2,'xl'=2,'ya'=2,'yb'=2,'yc'=2,'zh'=2,'zla'=2,'zlb'=2,'core'=2]..., dimensions={0} | all-to-all | bytes 229376 | tf_op jit(solution)/shard_map/all_to_all | solution.py:235
  39.6 16.4 %all_to_all.33 = f32[4,56,128]{2,1,0:T(8,128)S(1)} all-to-all(f32[4,56,128]{2,1,0:T(8,128)S(1)} %broadcast_in_dim.11), channel_id=1, replica_groups=mesh['xh'=2,'xl'=2,'ya'=2,'yb'=2,'yc'=2,'zh'=2,'zla'=2,'zlb'=2,'core'=2]..., dimensions={0} | all-to-all | bytes 229376 | tf_op jit(solution)/shard_map/all_to_all | solution.py:235
  56.0 11.2 %all_to_all.34 = f32[16,56,128]{2,1,0:T(8,128)S(1)} all-to-all(f32[16,56,128]{2,1,0:T(8,128)S(1)} %broadcast_in_dim.12), channel_id=1, replica_groups=mesh['xh'=2,'xl'=2,'ya'=2,'yb'=2,'yc'=2,'zh'=2,'zla'=2,'zlb'=2,'core'=2]..., dimensions={0} | all-to-all | bytes 917504 | tf_op jit(solution)/shard_map/all_to_all | solution.py:235
  67.2 0.1 broadcast_in_dim.14
  67.3 0.0 copy-start.1
  67.3 11.0 %all_to_all.35 = f32[2,896,128]{2,1,0:T(8,128)} all-to-all(f32[2,896,128]{2,1,0:T(8,128)S(1)} %broadcast_in_dim.14), channel_id=1, replica_groups=mesh['xh'=2,'xl'=2,'ya'=2,'yb'=2,'yc'=2,'zh'=2,'zla'=2,'zlb'=2,'core'=2]..., dimensions={0} | all-to-all | bytes 1835008 | tf_op jit(solution)/shard_map/all_to_all | solution.py:235
  78.3 0.0 copy-done.1
  78.3 2.3 %collective-permute-start = (f32[256,256]{1,0:T(8,128)S(1)}, f32[256,256]{1,0:T(8,128)S(1)}, u32[]{:S(2)}, u32[]{:S(2)}) collective-permute-start(f32[256,256]{1,0:T(8,128)S(1)} %copy-done.1), channel_id=1, source_target_pairs={{0,8},{8,16},{16,24},{24,32},{32,40},{40,48},{48,56},{56,64},{64,7... | collective-permute-start | bytes 786440 | tf_op jit(solution)/shard_map/ppermute | solution.py:231
  80.6 19.8 %shard_map.60 = (f32[2,256,256]{2,1,0:T(8,128)}, f32[2,256,256]{2,1,0:T(8,128)}) custom-call(f32[32,56,128]{2,1,0:T(8,128)} %bitcast.6), custom_call_target="tpu_custom_call" | custom-call | tf_op jit(solution)/shard_map/pallas_call | solution.py:220
  100.4 0.0 collective-permute-done.refs_6_
  100.4 0.0 copy-start
  100.4 0.7 copy-done
  101.1 5.9 %shard_map.61 = (f32[256,256]{1,0:T(8,128)}, f32[256,256]{1,0:T(8,128)}, f32[256,256]{1,0:T(8,128)}, f32[2,256,256]{2,1,0:T(8,128)}) custom-call(s32[2,2]{1,0:T(2,128)} %bitcast.12, f32[32,56,128]{2,1,0:T(8,128)} %bitcast.7, f32[2,256,256]{2,1,0:T(8,128)} %get-tuple-element.18.refs_2_, f32[2,256,256]{2,1,0:T(8,128)} %get-tuple-element.19.refs_3_, ...), custom_call_target="tpu_custom_call" | custom-call | tf_op jit(solution)/shard_map/pallas_call | solution.py:220
  107.0 7.0 %collective-permute-start.1 = (f32[256,256]{1,0:T(8,128)}, f32[256,256]{1,0:T(8,128)S(1)}, u32[]{:S(2)}, u32[]{:S(2)}) collective-permute-start(f32[256,256]{1,0:T(8,128)} %get-tuple-element.26), channel_id=1, source_target_pairs={{0,8},{8,16},{16,24},{24,32},{32,40},{40,48},{48,56},{56,64},{64,7... | collective-permute-start | bytes 786440 | tf_op jit(solution)/shard_map/ppermute | solution.py:231
  114.0 20.1 %shard_map.62 = (f32[256,256]{1,0:T(8,128)}, f32[256,256]{1,0:T(8,128)}) custom-call(f32[2,256,256]{2,1,0:T(8,128)} %get-tuple-element.22.gram_ref, f32[256,256]{1,0:T(8,128)} %get-tuple-element.23.source_ref, f32[256,256]{1,0:T(8,128)} %get-tuple-element.24.grad_ref), custom_call_target="tpu_custom_call" | custom-call | tf_op jit(solution)/shard_map/pallas_call | solution.py:220
  134.1 0.0 collective-permute-done.1
  134.1 1.9 %slice_subtract_fusion = f32[128,256]{1,0:T(8,128)} fusion(f32[256,256]{1,0:T(8,128)S(1)} %collective-permute-done.1, f32[256,256]{1,0:T(8,128)} %get-tuple-element.27), kind=kOutput, calls=%fused_computation.2 | convolution fusion | flops 100728832 | bytes 655360 | tf_op jit(solution)/shard_map/dot_general | solution.py:20
  (6 shorter events, 0.1 us)
Async XLA Ops:
  67.3 11.0 %copy-start.1 = (f32[256,256]{1,0:T(8,128)S(1)}, f32[256,256]{1,0:T(8,128)}, u32[]{:S(2)}) copy-start(f32[256,256]{1,0:T(8,128)} %get-tuple-element.21) | copy-start | bytes 786436
  78.3 22.1 %collective-permute-start = (f32[256,256]{1,0:T(8,128)S(1)}, f32[256,256]{1,0:T(8,128)S(1)}, u32[]{:S(2)}, u32[]{:S(2)}) collective-permute-start(f32[256,256]{1,0:T(8,128)S(1)} %copy-done.1), channel_id=1, source_target_pairs={{0,8},{8,16},{16,24},{24,32},{32,40},{40,48},{48,56},{56,64},{64,7... | collective-permute-start | bytes 786440 | tf_op jit(solution)/shard_map/ppermute | solution.py:231
  100.4 0.7 copy-start
  107.0 27.2 %collective-permute-start.1 = (f32[256,256]{1,0:T(8,128)}, f32[256,256]{1,0:T(8,128)S(1)}, u32[]{:S(2)}, u32[]{:S(2)}) collective-permute-start(f32[256,256]{1,0:T(8,128)} %get-tuple-element.26), channel_id=1, source_target_pairs={{0,8},{8,16},{16,24},{24,32},{32,40},{40,48},{48,56},{56,64},{64,7... | collective-permute-start | bytes 786440 | tf_op jit(solution)/shard_map/ppermute | solution.py:231

commit v4 on v3

--- a/solution.py
+++ b/solution.py
@@ -14,14 +14,16 @@
 FAR = (("ya", "yb"), ("zh", "zla"))
 PIECES = 32
 BLOCK = 64
-
-
-def product(left, right, left_dim, right_dim):
+TURNS = 4
+RESIDUAL = 0.003
+
+
+def product(left, right, left_dim, right_dim, precision=lax.Precision.HIGHEST):
     return lax.dot_general(
         left,
         right,
         (((left_dim,), (right_dim,)), ((), ())),
-        precision=lax.Precision.HIGHEST,
+        precision=precision,
         preferred_element_type=jnp.float32,
     )
 
@@ -207,9 +209,46 @@
     gram_out[1] = updated_gram(gram_ref[1], cross.T, square_target, inverse_ref[0]) / target_rows
 
 
-def third_kernel(gram_ref, source_ref, grad_ref, source_out, inverse_out, work):
-    work[...] = gram_ref[...]
-    invert_pair(work)
+def invert_pair_from(gram_ref, guess_ref, inverse_ref, error_ref):
+    size = gram_ref.shape[1]
+    row, col = grid_of((size, size))
+
+    def residual():
+        total = 0.0
+        for t in range(2):
+            error = jnp.where(row == col, 1.0, 0.0) - product(gram_ref[t], inverse_ref[t], 1, 0)
+            error_ref[t] = error
+            total += jnp.sum(error * error)
+        return total
+
+    def refine():
+        for t in range(2):
+            error = error_ref[t]
+            error += product(error, error, 1, 0, lax.Precision.DEFAULT)
+            inverse_ref[t] += product(inverse_ref[t], error, 1, 0)
+
+    def turn(state):
+        refine()
+        return state[0] + 1, residual()
+
+    inverse_ref[...] = guess_ref[...]
+    _, total = lax.while_loop(
+        lambda state: (state[0] < TURNS) & (state[1] > RESIDUAL * RESIDUAL), turn, (0, residual())
+    )
+    settled = total <= RESIDUAL * RESIDUAL
+
+    @pl.when(settled)
+    def _():
+        refine()
+
+    @pl.when(jnp.logical_not(settled))
+    def _():
+        inverse_ref[...] = gram_ref[...]
+        invert_pair(inverse_ref)
+
+
+def third_kernel(gram_ref, guess_ref, source_ref, grad_ref, source_out, inverse_out, work, error):
+    invert_pair_from(gram_ref, guess_ref, work, error)
     source_out[...] = source_ref[...] - step_size * product(grad_ref[...], work[1], 1, 0)
     inverse_out[...] = work[0]
 
@@ -270,7 +309,7 @@
         flags, sums, grams, inverse, source, grad, moving, observed, scalars=1,
     )
     moving = next_position(moving)
-    source, inverse = call(third_kernel, (square, square), ((2, *square),), grams, source, grad)
+    source, inverse = call(third_kernel, (square, square), (pair, pair), grams, inverse, source, grad)
     count = target.shape[0]
     target = moving[:count] - step_size * product(moving[count:], inverse, 1, 0)
     return source, target

time: 137 us -> 130 us (0.949)
  Pallas kernels: 49.8 us -> 38.6 us
  waiting for transfers between devices: 0.01 us -> 4.64 us
    pallas_call x4, Pallas kernels: 49.8 us -> 38.6 us  [call(): pl.pallas_call(kernel, out_shape=[jax.ShapeDtypeStruct(shape, jnp.float32...]
    ppermute x2, waiting for transfers between devices: 0.01 us -> 4.64 us  [next_position(): lax.ppermute(value, WIDE, [(place, (place + 1) % count) for place in rang...]
  transfers between devices with their start and end apart: 2 -> 2, of which waited for: 0 -> 1; matrix products, arithmetic and copies ran while one was open for 0% -> 0% of each run, Pallas kernels for 29% -> 22%
where the time goes in v4:
time: 130 us
  blocking collectives  73.4 us (56%)
  Pallas kernels  38.6 us (30%)
  starting transfers between devices  9.29 us (7%)
  waiting for transfers between devices  4.64 us (4%)
  matrix products  1.89 us (1%)
    all_to_all x6, blocking collectives, exchanged(): return lax.all_to_all(value, axes, 0, 0, tiled=True)  73.4 us
    pallas_call x4, Pallas kernels, call(): pl.pallas_call(kernel, out_shape=[jax.ShapeDtypeStruct(shape, jnp.float32...  38.6 us
    ppermute x2, starting transfers between devices, next_position(): lax.ppermute(value, WIDE, [(place, (place + 1) % count) for place in rang...  9.29 us
    ppermute x2, waiting for transfers between devices, next_position(): lax.ppermute(value, WIDE, [(place, (place + 1) % count) for place in rang...  4.64 us
  transfers between devices with their start and end apart: 2, of which 1 were waited for; matrix products, arithmetic and copies ran while one was open for 0% of the time, Pallas kernels for 22%

profile of v4, /device:TPU:1, one launch (start us, length us, event | category | flops | bytes accessed | tf_op | source)
XLA Modules:
  0.0 129.5 jit_solution(7261059543897001016)
XLA Ops:
  0.6 4.0 %shard_map.59 = (f32[256,256]{1,0:T(8,128)}, f32[256,256]{1,0:T(8,128)}, f32[32,56,128]{2,1,0:T(8,128)}) custom-call(s32[2,2]{1,0:T(2,128)} %bitcast.11, f32[256,256]{1,0:T(8,128)} %refs_4_.1, f32[128,256]{1,0:T(8,128)} %target_ref.1, f32[2,256,128]{2,1,0:T(8,128)} %refs_7_.1), custom_call_target="tpu_custom_call" | custom-call | tf_op jit(solution)/shard_map/pallas_call | solution.py:259
  4.6 12.0 %all_to_all.30 = f32[2,896,128]{2,1,0:T(8,128)S(1)} all-to-all(f32[2,896,128]{2,1,0:T(8,128)} %bitcast.10), channel_id=1, replica_groups=mesh['xh'=2,'xl'=2,'ya'=2,'yb'=2,'yc'=2,'zh'=2,'zla'=2,'zlb'=2,'core'=2]..., dimensions={0} | all-to-all | bytes 1835008 | tf_op jit(solution)/shard_map/all_to_all | solution.py:274
  16.6 0.1 reduce_sum.36
  16.7 11.6 %all_to_all.31 = f32[16,56,128]{2,1,0:T(8,128)S(1)} all-to-all(f32[16,56,128]{2,1,0:T(8,128)S(1)} %bitcast.8), channel_id=1, replica_groups=mesh['xh'=2,'xl'=2,'ya'=2,'yb'=2,'yc'=2,'zh'=2,'zla'=2,'zlb'=2,'core'=2]..., dimensions={0} | all-to-all | bytes 917504 | tf_op jit(solution)/shard_map/all_to_all | solution.py:274
  28.4 11.2 %all_to_all.32 = f32[4,56,128]{2,1,0:T(8,128)S(1)} all-to-all(f32[4,56,128]{2,1,0:T(8,128)S(1)} %broadcast_in_dim.10), channel_id=1, replica_groups=mesh['xh'=2,'xl'=2,'ya'=2,'yb'=2,'yc'=2,'zh'=2,'zla'=2,'zlb'=2,'core'=2]..., dimensions={0} | all-to-all | bytes 229376 | tf_op jit(solution)/shard_map/all_to_all | solution.py:274
  39.6 16.4 %all_to_all.33 = f32[4,56,128]{2,1,0:T(8,128)S(1)} all-to-all(f32[4,56,128]{2,1,0:T(8,128)S(1)} %broadcast_in_dim.11), channel_id=1, replica_groups=mesh['xh'=2,'xl'=2,'ya'=2,'yb'=2,'yc'=2,'zh'=2,'zla'=2,'zlb'=2,'core'=2]..., dimensions={0} | all-to-all | bytes 229376 | tf_op jit(solution)/shard_map/all_to_all | solution.py:274
  56.0 11.2 %all_to_all.34 = f32[16,56,128]{2,1,0:T(8,128)S(1)} all-to-all(f32[16,56,128]{2,1,0:T(8,128)S(1)} %broadcast_in_dim.12), channel_id=1, replica_groups=mesh['xh'=2,'xl'=2,'ya'=2,'yb'=2,'yc'=2,'zh'=2,'zla'=2,'zlb'=2,'core'=2]..., dimensions={0} | all-to-all | bytes 917504 | tf_op jit(solution)/shard_map/all_to_all | solution.py:274
  67.2 0.1 broadcast_in_dim.14
  67.3 0.0 copy-start.1
  67.3 11.0 %all_to_all.35 = f32[2,896,128]{2,1,0:T(8,128)} all-to-all(f32[2,896,128]{2,1,0:T(8,128)S(1)} %broadcast_in_dim.14), channel_id=1, replica_groups=mesh['xh'=2,'xl'=2,'ya'=2,'yb'=2,'yc'=2,'zh'=2,'zla'=2,'zlb'=2,'core'=2]..., dimensions={0} | all-to-all | bytes 1835008 | tf_op jit(solution)/shard_map/all_to_all | solution.py:274
  78.3 0.0 copy-done.1
  78.3 2.3 %collective-permute-start = (f32[256,256]{1,0:T(8,128)S(1)}, f32[256,256]{1,0:T(8,128)S(1)}, u32[]{:S(2)}, u32[]{:S(2)}) collective-permute-start(f32[256,256]{1,0:T(8,128)S(1)} %copy-done.1), channel_id=1, source_target_pairs={{0,8},{8,16},{16,24},{24,32},{32,40},{40,48},{48,56},{56,64},{64,7... | collective-permute-start | bytes 786440 | tf_op jit(solution)/shard_map/ppermute | solution.py:270
  80.6 19.7 %shard_map.60 = (f32[2,256,256]{2,1,0:T(8,128)}, f32[2,256,256]{2,1,0:T(8,128)}) custom-call(f32[32,56,128]{2,1,0:T(8,128)} %bitcast.6), custom_call_target="tpu_custom_call" | custom-call | tf_op jit(solution)/shard_map/pallas_call | solution.py:259
  100.3 0.0 collective-permute-done.refs_6_
  100.3 0.0 copy-start
  100.4 0.7 copy-done
  101.1 5.9 %shard_map.61 = (f32[256,256]{1,0:T(8,128)}, f32[256,256]{1,0:T(8,128)}, f32[256,256]{1,0:T(8,128)}, f32[2,256,256]{2,1,0:T(8,128)}) custom-call(s32[2,2]{1,0:T(2,128)} %bitcast.12, f32[32,56,128]{2,1,0:T(8,128)} %bitcast.7, f32[2,256,256]{2,1,0:T(8,128)} %get-tuple-element.18.refs_2_, f32[2,256,256]{2,1,0:T(8,128)} %get-tuple-element.19.refs_3_.guess_ref, ...), custom_call_target="tpu_custom_call" | custom-call | tf_op jit(solution)/shard_map/pallas_call | solution.py:259
  106.9 7.0 %collective-permute-start.1 = (f32[256,256]{1,0:T(8,128)}, f32[256,256]{1,0:T(8,128)S(1)}, u32[]{:S(2)}, u32[]{:S(2)}) collective-permute-start(f32[256,256]{1,0:T(8,128)} %get-tuple-element.26), channel_id=1, source_target_pairs={{0,8},{8,16},{16,24},{24,32},{32,40},{40,48},{48,56},{56,64},{64,7... | collective-permute-start | bytes 786440 | tf_op jit(solution)/shard_map/ppermute | solution.py:270
  114.0 9.0 %shard_map.62 = (f32[256,256]{1,0:T(8,128)}, f32[256,256]{1,0:T(8,128)}) custom-call(f32[2,256,256]{2,1,0:T(8,128)} %get-tuple-element.22.gram_ref, f32[2,256,256]{2,1,0:T(8,128)} %get-tuple-element.19.refs_3_.guess_ref, f32[256,256]{1,0:T(8,128)} %get-tuple-element.23.source_ref, f32[256,256]{1,0:T(8,128)} %get-tuple-element.24.grad_ref), custom_call_target="tpu_custom_call" | custom-call | tf_op jit(solution)/shard_map/pallas_call | solution.py:259
  123.0 4.6 %collective-permute-done.1 = f32[256,256]{1,0:T(8,128)S(1)} collective-permute-done((f32[256,256]{1,0:T(8,128)}, f32[256,256]{1,0:T(8,128)S(1)}, u32[]{:S(2)}, u32[]{:S(2)}) %collective-permute-start.1) | collective-permute-done | bytes 262176 | tf_op jit(solution)/shard_map/ppermute | solution.py:270
  127.6 1.9 %slice_subtract_fusion = f32[128,256]{1,0:T(8,128)} fusion(f32[256,256]{1,0:T(8,128)S(1)} %collective-permute-done.1, f32[256,256]{1,0:T(8,128)} %get-tuple-element.27), kind=kOutput, calls=%fused_computation.2 | convolution fusion | flops 100728832 | bytes 655360 | tf_op jit(solution)/shard_map/dot_general | solution.py:22
  (6 shorter events, 0.1 us)
Async XLA Ops:
  67.3 11.0 %copy-start.1 = (f32[256,256]{1,0:T(8,128)S(1)}, f32[256,256]{1,0:T(8,128)}, u32[]{:S(2)}) copy-start(f32[256,256]{1,0:T(8,128)} %get-tuple-element.21) | copy-start | bytes 786436
  78.3 22.0 %collective-permute-start = (f32[256,256]{1,0:T(8,128)S(1)}, f32[256,256]{1,0:T(8,128)S(1)}, u32[]{:S(2)}, u32[]{:S(2)}) collective-permute-start(f32[256,256]{1,0:T(8,128)S(1)} %copy-done.1), channel_id=1, source_target_pairs={{0,8},{8,16},{16,24},{24,32},{32,40},{40,48},{48,56},{56,64},{64,7... | collective-permute-start | bytes 786440 | tf_op jit(solution)/shard_map/ppermute | solution.py:270
  100.3 0.7 copy-start
  106.9 20.7 %collective-permute-start.1 = (f32[256,256]{1,0:T(8,128)}, f32[256,256]{1,0:T(8,128)S(1)}, u32[]{:S(2)}, u32[]{:S(2)}) collective-permute-start(f32[256,256]{1,0:T(8,128)} %get-tuple-element.26), channel_id=1, source_target_pairs={{0,8},{8,16},{16,24},{24,32},{32,40},{40,48},{48,56},{56,64},{64,7... | collective-permute-start | bytes 786440 | tf_op jit(solution)/shard_map/ppermute | solution.py:270

commit v5 on v4

--- a/solution.py
+++ b/solution.py
@@ -119,11 +119,10 @@
         ref[t, half:, half:] = trailing[t] * across[:, half:] * down[half:]
 
 
-def gradients(source, target, observed, upper, lower):
+def masked_residual(source, target, observed, upper, lower):
     row = lax.broadcasted_iota(jnp.int32, observed.shape, 0)
     mask = jnp.where(row < observed.shape[0] // 2, upper, lower).astype(jnp.float32)
-    residual = mask * (product(source, target, 1, 1) - observed)
-    return product(residual, target, 1, 0), product(residual, source, 0, 0)
+    return mask * (product(source, target, 1, 1) - observed)
 
 
 def diagonal(square):
@@ -134,7 +133,8 @@
 def first_kernel(tiles, source_ref, target_ref, observed_ref, grad_ref, moving_ref, sums_ref):
     source, target = source_ref[...], target_ref[...]
     count = target.shape[0]
-    grad_source, grad_target = gradients(source, target, observed_ref[0], tiles[0, 0], tiles[0, 1])
+    residual = masked_residual(source, target, observed_ref[0], tiles[0, 0], tiles[0, 1])
+    grad_source, grad_target = product(residual, target, 1, 0), product(residual, source, 0, 0)
     grad_ref[...] = grad_source
     moving_ref[:count, :] = target
     moving_ref[count:, :] = grad_target
@@ -183,30 +183,25 @@
     return gram - step_size * (moved + moved.T) + (step_size * step_size) * twice
 
 
-def inverse_kernel(source_rows, target_rows, sums_ref, gram_out, inverse_out):
+def inverse_kernel(source_rows, target_rows, sums_ref, source_ref, grad_ref, gram_out, inverse_out, source_out):
     gram_out[0], gram_out[1] = unpacked_pair(sums_ref, 1)
     inverse_out[0] = gram_out[0] / source_rows
     inverse_out[1] = gram_out[1] / target_rows
     invert_pair(inverse_out)
-
-
-def second_kernel(
-    source_rows, target_rows,
-    tiles, sums_ref, gram_ref, inverse_ref, source_ref, grad_ref, moving_ref, observed_ref,
-    source_out, grad_out, moving_out, gram_out,
-):
+    source_out[...] = source_ref[...] - step_size * product(grad_ref[...], inverse_out[1], 1, 0)
+
+
+def target_step(moving_ref, inverse):
     count = moving_ref.shape[0] // 2
-    source = source_ref[...] - step_size * product(grad_ref[...], inverse_ref[1], 1, 0)
-    target = moving_ref[:count, :] - step_size * product(moving_ref[count:, :], inverse_ref[0], 1, 0)
-    source_out[...] = source
-    moving_out[:count, :] = target
-    grad_source, grad_target = gradients(source, target, observed_ref[1], tiles[1, 0], tiles[1, 1])
-    grad_out[...] = grad_source
-    moving_out[count:, :] = grad_target
-    square_source, square_target = unpacked_pair(sums_ref, 2)
-    cross = unpacked(sums_ref, 0)
-    gram_out[0] = updated_gram(gram_ref[0], cross, square_source, inverse_ref[1]) / source_rows
-    gram_out[1] = updated_gram(gram_ref[1], cross.T, square_target, inverse_ref[0]) / target_rows
+    return moving_ref[:count, :] - step_size * product(moving_ref[count:, :], inverse, 1, 0)
+
+
+def second_kernel(tiles, inverse_ref, source_ref, moving_ref, observed_ref, target_out, residual_out, grad_out):
+    target = target_step(moving_ref, inverse_ref[0])
+    residual = masked_residual(source_ref[...], target, observed_ref[1], tiles[1, 0], tiles[1, 1])
+    grad_out[...] = product(residual, source_ref[...], 0, 0)
+    target_out[...] = target
+    residual_out[...] = residual
 
 
 def invert_pair_from(gram_ref, guess_ref, inverse_ref, error_ref):
@@ -247,10 +242,21 @@
         invert_pair(inverse_ref)
 
 
-def third_kernel(gram_ref, guess_ref, source_ref, grad_ref, source_out, inverse_out, work, error):
-    invert_pair_from(gram_ref, guess_ref, work, error)
-    source_out[...] = source_ref[...] - step_size * product(grad_ref[...], work[1], 1, 0)
-    inverse_out[...] = work[0]
+def third_kernel(
+    source_rows, target_rows,
+    sums_ref, gram_ref, inverse_ref, source_ref, target_ref, residual_ref, leaving_ref,
+    source_out, tail_out, moved, work, error,
+):
+    square_source, square_target = unpacked_pair(sums_ref, 2)
+    cross = unpacked(sums_ref, 0)
+    moved[0] = updated_gram(gram_ref[0], cross, square_source, inverse_ref[1]) / source_rows
+    moved[1] = updated_gram(gram_ref[1], cross.T, square_target, inverse_ref[0]) / target_rows
+    invert_pair_from(moved, inverse_ref, work, error)
+    grad = product(residual_ref[...], target_ref[...], 1, 0)
+    source_out[...] = source_ref[...] - step_size * product(grad, work[1], 1, 0)
+    count = target_ref.shape[0]
+    tail_out[:count, :] = target_step(leaving_ref, inverse_ref[0])
+    tail_out[count:, :] = -step_size * work[0]
 
 
 def call(kernel, shapes, scratch, *arguments, scalars=0):
@@ -265,9 +271,9 @@
     )(*arguments)
 
 
-def next_position(value):
+def moved_on(value, steps):
     count = lax.axis_size(WIDE)
-    return lax.ppermute(value, WIDE, [(place, (place + 1) % count) for place in range(count)])
+    return lax.ppermute(value, WIDE, [(place, (place + steps) % count) for place in range(count)])
 
 
 def exchanged(value, axes):
@@ -294,25 +300,27 @@
         sums = jnp.sum(spread(sums, axes), axis=0)
     sums = spread(sums, NEAR).reshape(-1, 128)
     sums, moving = lax.optimization_barrier((spread(sums, "core").reshape(shape), moving))
-    moving = next_position(moving)
+    leaving = moved_on(moving, 2)
+    moving = moved_on(moving, 1)
 
     def inverses(*refs):
         inverse_kernel(source_rows, target_rows, *refs)
 
-    def middle(*refs):
-        second_kernel(source_rows, target_rows, *refs)
+    def final(*refs):
+        third_kernel(source_rows, target_rows, *refs)
 
     pair = (2, *square)
-    grams, inverse = call(inverses, (pair, pair), (), sums)
-    source, grad, moving, grams = call(
-        middle, (square, square, square, pair), (),
-        flags, sums, grams, inverse, source, grad, moving, observed, scalars=1,
-    )
-    moving = next_position(moving)
-    source, inverse = call(third_kernel, (square, square), (pair, pair), grams, inverse, source, grad)
-    count = target.shape[0]
-    target = moving[:count] - step_size * product(moving[count:], inverse, 1, 0)
-    return source, target
+    grams, inverse, source = call(inverses, (pair, pair, square), (), sums, source, grad)
+    block = target.shape
+    target, residual, grad = call(
+        second_kernel, (block, (block[1], block[0]), block), (), flags, inverse, source, moving, observed, scalars=1
+    )
+    grad = moved_on(grad, 1)
+    count = block[0]
+    source, tail = call(
+        final, (square, (count + 256, 256)), (pair, pair, pair), sums, grams, inverse, source, target, residual, leaving
+    )
+    return source, tail[:count] + product(grad, tail[count:], 1, 0)
 
 
 def solution(mesh):

time: 130 us -> 130 us (level)
  waiting for transfers between devices: 4.64 us -> 0.01 us
  Pallas kernels: 38.6 us -> 41.1 us
  starting transfers between devices: 9.29 us -> 11.2 us
    ppermute x2 -> x3, waiting for transfers between devices: 4.64 us -> 0.01 us  [moved_on(): lax.ppermute(value, WIDE, [(place, (place + steps) % count) for place in...]
    pallas_call x4, Pallas kernels: 38.6 us -> 41.1 us  [call(): pl.pallas_call(kernel, out_shape=[jax.ShapeDtypeStruct(shape, jnp.float32...]
    ppermute x2 -> x3, starting transfers between devices: 9.29 us -> 11.2 us  [moved_on(): lax.ppermute(value, WIDE, [(place, (place + steps) % count) for place in...]
  transfers between devices with their start and end apart: 2 -> 3, of which waited for: 1 -> 0; matrix products, arithmetic and copies ran while one was open for 0% -> 0% of each run, Pallas kernels for 22% -> 29%
where the time goes in v5:
time: 130 us
  blocking collectives  73.4 us (56%)
  Pallas kernels  41.1 us (32%)
  starting transfers between devices  11.2 us (9%)
  matrix products  1.92 us (1%)
  local copies, waits for them, and re-layouts  1.51 us (1%)
    all_to_all x6, blocking collectives, exchanged(): return lax.all_to_all(value, axes, 0, 0, tiled=True)  73.4 us
    pallas_call x4, Pallas kernels, call(): pl.pallas_call(kernel, out_shape=[jax.ShapeDtypeStruct(shape, jnp.float32...  41.1 us
    ppermute x3, starting transfers between devices, moved_on(): lax.ppermute(value, WIDE, [(place, (place + steps) % count) for place in...  11.2 us
  transfers between devices with their start and end apart: 3, of which 0 were waited for; matrix products, arithmetic and copies ran while one was open for 0% of the time, Pallas kernels for 29%

profile of v5, /device:TPU:1, one launch (start us, length us, event | category | flops | bytes accessed | tf_op | source)
XLA Modules:
  0.0 130.0 jit_solution(17052467269473133684)
XLA Ops:
  0.6 4.0 %shard_map.59 = (f32[256,256]{1,0:T(8,128)}, f32[256,256]{1,0:T(8,128)}, f32[32,56,128]{2,1,0:T(8,128)}) custom-call(s32[2,2]{1,0:T(2,128)} %bitcast.11, f32[256,256]{1,0:T(8,128)} %refs_1_.1, f32[128,256]{1,0:T(8,128)} %target_ref.1, f32[2,256,128]{2,1,0:T(8,128)} %observed_ref.3), custom_call_target="tpu_custom_call" | custom-call | tf_op jit(solution)/shard_map/pallas_call | solution.py:265
  4.6 12.0 %all_to_all.30 = f32[2,896,128]{2,1,0:T(8,128)S(1)} all-to-all(f32[2,896,128]{2,1,0:T(8,128)} %bitcast.10), channel_id=1, replica_groups=mesh['xh'=2,'xl'=2,'ya'=2,'yb'=2,'yc'=2,'zh'=2,'zla'=2,'zlb'=2,'core'=2]..., dimensions={0} | all-to-all | bytes 1835008 | tf_op jit(solution)/shard_map/all_to_all | solution.py:280
  16.6 0.1 reduce_sum.36
  16.7 11.6 %all_to_all.31 = f32[16,56,128]{2,1,0:T(8,128)S(1)} all-to-all(f32[16,56,128]{2,1,0:T(8,128)S(1)} %bitcast.8), channel_id=1, replica_groups=mesh['xh'=2,'xl'=2,'ya'=2,'yb'=2,'yc'=2,'zh'=2,'zla'=2,'zlb'=2,'core'=2]..., dimensions={0} | all-to-all | bytes 917504 | tf_op jit(solution)/shard_map/all_to_all | solution.py:280
  28.4 11.2 %all_to_all.32 = f32[4,56,128]{2,1,0:T(8,128)S(1)} all-to-all(f32[4,56,128]{2,1,0:T(8,128)S(1)} %broadcast_in_dim.10), channel_id=1, replica_groups=mesh['xh'=2,'xl'=2,'ya'=2,'yb'=2,'yc'=2,'zh'=2,'zla'=2,'zlb'=2,'core'=2]..., dimensions={0} | all-to-all | bytes 229376 | tf_op jit(solution)/shard_map/all_to_all | solution.py:280
  39.6 16.4 %all_to_all.33 = f32[4,56,128]{2,1,0:T(8,128)S(1)} all-to-all(f32[4,56,128]{2,1,0:T(8,128)S(1)} %broadcast_in_dim.11), channel_id=1, replica_groups=mesh['xh'=2,'xl'=2,'ya'=2,'yb'=2,'yc'=2,'zh'=2,'zla'=2,'zlb'=2,'core'=2]..., dimensions={0} | all-to-all | bytes 229376 | tf_op jit(solution)/shard_map/all_to_all | solution.py:280
  56.0 11.2 %all_to_all.34 = f32[16,56,128]{2,1,0:T(8,128)S(1)} all-to-all(f32[16,56,128]{2,1,0:T(8,128)S(1)} %broadcast_in_dim.12), channel_id=1, replica_groups=mesh['xh'=2,'xl'=2,'ya'=2,'yb'=2,'yc'=2,'zh'=2,'zla'=2,'zlb'=2,'core'=2]..., dimensions={0} | all-to-all | bytes 917504 | tf_op jit(solution)/shard_map/all_to_all | solution.py:280
  67.2 0.1 broadcast_in_dim.14
  67.3 0.0 copy-start.2
  67.3 11.0 %all_to_all.35 = f32[2,896,128]{2,1,0:T(8,128)} all-to-all(f32[2,896,128]{2,1,0:T(8,128)S(1)} %broadcast_in_dim.14), channel_id=1, replica_groups=mesh['xh'=2,'xl'=2,'ya'=2,'yb'=2,'yc'=2,'zh'=2,'zla'=2,'zlb'=2,'core'=2]..., dimensions={0} | all-to-all | bytes 1835008 | tf_op jit(solution)/shard_map/all_to_all | solution.py:280
  78.3 0.0 copy-done.2
  78.3 2.3 %collective-permute-start = (f32[256,256]{1,0:T(8,128)S(1)}, f32[256,256]{1,0:T(8,128)S(1)}, u32[]{:S(2)}, u32[]{:S(2)}) collective-permute-start(f32[256,256]{1,0:T(8,128)S(1)} %copy-done.2), channel_id=1, source_target_pairs={{0,8},{8,16},{16,24},{24,32},{32,40},{40,48},{48,56},{56,64},{64,7... | collective-permute-start | bytes 786440 | tf_op jit(solution)/shard_map/ppermute | solution.py:276
  80.6 2.3 %collective-permute-start.1 = (f32[256,256]{1,0:T(8,128)S(1)}, f32[256,256]{1,0:T(8,128)S(1)}, u32[]{:S(2)}, u32[]{:S(2)}) collective-permute-start(f32[256,256]{1,0:T(8,128)S(1)} %copy-done.2), channel_id=1, source_target_pairs={{0,16},{8,24},{16,32},{24,40},{32,48},{40,56},{48,64},{56,72},{64,... | collective-permute-start | bytes 786440 | tf_op jit(solution)/shard_map/ppermute | solution.py:276
  82.9 20.5 %shard_map.60 = (f32[2,256,256]{2,1,0:T(8,128)}, f32[2,256,256]{2,1,0:T(8,128)}, f32[256,256]{1,0:T(8,128)}) custom-call(f32[32,56,128]{2,1,0:T(8,128)} %bitcast.6, f32[256,256]{1,0:T(8,128)} %refs_1_.1, f32[256,256]{1,0:T(8,128)} %get-tuple-element.18.refs_2_), custom_call_target="tpu_custom_call" | custom-call | tf_op jit(solution)/shard_map/pallas_call | solution.py:265
  103.4 0.0 collective-permute-done.moving_ref
  103.4 0.0 copy-start
  103.4 0.7 copy-done
  104.1 3.2 %shard_map.61 = (f32[128,256]{1,0:T(8,128)}, f32[256,128]{1,0:T(8,128)}, f32[128,256]{1,0:T(8,128)}) custom-call(s32[2,2]{1,0:T(2,128)} %bitcast.12, f32[2,256,256]{2,1,0:T(8,128)} %get-tuple-element.20.inverse_ref.refs_2_, f32[256,256]{1,0:T(8,128)} %get-tuple-element.21.source_ref.refs_3_, f32[256,256]{1,0:T(8,128)} %copy-done, f32[2,256,128]{2,1,0:T(8,128)} %observed_ref.3), custom_call_target="tpu_custom_call" | custom-call | tf_op jit(solution)/shard_map/pallas_call | solution.py:265
  107.3 6.6 %collective-permute-start.2 = (f32[128,256]{1,0:T(8,128)}, f32[128,256]{1,0:T(8,128)S(1)}, u32[]{:S(2)}, u32[]{:S(2)}) collective-permute-start(f32[128,256]{1,0:T(8,128)} %get-tuple-element.27), channel_id=1, source_target_pairs={{0,8},{8,16},{16,24},{24,32},{32,40},{40,48},{48,56},{56,64},{64,7... | collective-permute-start | bytes 393224 | tf_op jit(solution)/shard_map/ppermute | solution.py:276
  113.9 0.0 collective-permute-done.1.refs_6_
  113.9 0.0 copy-start.1
  113.9 0.7 copy-done.1
  114.6 13.5 %shard_map.62 = (f32[256,256]{1,0:T(8,128)}, f32[384,256]{1,0:T(8,128)}) custom-call(f32[32,56,128]{2,1,0:T(8,128)} %bitcast.7, f32[2,256,256]{2,1,0:T(8,128)} %get-tuple-element.19.refs_1_, f32[2,256,256]{2,1,0:T(8,128)} %get-tuple-element.20.inverse_ref.refs_2_, f32[256,256]{1,0:T(8,128)} %get-tuple-element.21.source_ref.refs_3_, ...), custom_call_target="tpu_custom_call" | custom-call | tf_op jit(solution)/shard_map/pallas_call | solution.py:265
  128.1 0.0 collective-permute-done.2
  128.1 1.9 %slice_add_fusion = f32[128,256]{1,0:T(8,128)} fusion(f32[384,256]{1,0:T(8,128)} %get-tuple-element.26, f32[128,256]{1,0:T(8,128)S(1)} %collective-permute-done.2), kind=kOutput, calls=%fused_computation.2 | convolution fusion | flops 100696064 | bytes 655360 | tf_op jit(solution)/shard_map/dot_general | solution.py:22
  (6 shorter events, 0.1 us)
Async XLA Ops:
  67.3 11.0 %copy-start.2 = (f32[256,256]{1,0:T(8,128)S(1)}, f32[256,256]{1,0:T(8,128)}, u32[]{:S(2)}) copy-start(f32[256,256]{1,0:T(8,128)} %get-tuple-element.22) | copy-start | bytes 786436
  78.3 25.1 %collective-permute-start = (f32[256,256]{1,0:T(8,128)S(1)}, f32[256,256]{1,0:T(8,128)S(1)}, u32[]{:S(2)}, u32[]{:S(2)}) collective-permute-start(f32[256,256]{1,0:T(8,128)S(1)} %copy-done.2), channel_id=1, source_target_pairs={{0,8},{8,16},{16,24},{24,32},{32,40},{40,48},{48,56},{56,64},{64,7... | collective-permute-start | bytes 786440 | tf_op jit(solution)/shard_map/ppermute | solution.py:276
  80.6 33.3 %collective-permute-start.1 = (f32[256,256]{1,0:T(8,128)S(1)}, f32[256,256]{1,0:T(8,128)S(1)}, u32[]{:S(2)}, u32[]{:S(2)}) collective-permute-start(f32[256,256]{1,0:T(8,128)S(1)} %copy-done.2), channel_id=1, source_target_pairs={{0,16},{8,24},{16,32},{24,40},{32,48},{40,56},{48,64},{56,72},{64,... | collective-permute-start | bytes 786440 | tf_op jit(solution)/shard_map/ppermute | solution.py:276
  103.4 0.7 copy-start
  107.3 20.8 %collective-permute-start.2 = (f32[128,256]{1,0:T(8,128)}, f32[128,256]{1,0:T(8,128)S(1)}, u32[]{:S(2)}, u32[]{:S(2)}) collective-permute-start(f32[128,256]{1,0:T(8,128)} %get-tuple-element.27), channel_id=1, source_target_pairs={{0,8},{8,16},{16,24},{24,32},{32,40},{40,48},{48,56},{56,64},{64,7... | collective-permute-start | bytes 393224 | tf_op jit(solution)/shard_map/ppermute | solution.py:276
  113.9 0.7 copy-start.1
